TPU v7x, 256 devices: a whole 4x4x8 slice. The times are simulated.
256 devices in a mesh: seq: 8 (over y, x_lo), rep: 16 (over z, core), exp: 2 (over x_hi).
Axes of the slice: x: 4 (x_hi: 2, x_lo: 2; x = x_hi * 2 + x_lo), y: 4, z: 8, core: 2. Of those that a mesh axis runs over, the one named last changes fastest.
Arguments:
- residual_in: bfloat16 [32, 1024, 2048], P(('rep', 'exp'), 'seq'), may hold values from -40 to 40
- queries: bfloat16 [32, 1024, 2048], P(('rep', 'exp'), 'seq'), may hold values from -6 to 6
- key_feats: bfloat16 [32, 1024, 2048], P(('rep', 'exp'), 'seq'), may hold values from -0.5390625 to 0.5390625
- value_feats: bfloat16 [32, 1024, 2048], P(('rep', 'exp'), 'seq'), may hold values from -6 to 6
- log_decay: float32 [32, 16, 1024], P(('rep', 'exp'), None, 'seq'), may hold values from -1.3 to 0
- out_cotangent: bfloat16 [32, 8, 32, 2048], P(('rep', 'exp'), 'seq'), may hold values from -6 to 6
- mask_pos: int32 [32, 8, 32], P(('rep', 'exp'), 'seq'), may hold values from 0 to 127, as said below
- route_rows: int32 [32, 8, 2, 128], P(('rep', 'exp'), 'seq'), may hold values from 0 to 127, as said below
- route_weight: float32 [32, 8, 2, 128], P(('rep', 'exp'), 'seq'), may hold values from 0.2 to 1
- up_proj: bfloat16 [2, 2048, 768], P('exp', ('seq', 'rep')), may hold values from -0.125 to 0.125
- down_proj: bfloat16 [2, 2048, 768], P('exp', ('seq', 'rep')), may hold values from -0.21875 to 0.21875
Outputs:
- query_grad: bfloat16 [32, 1024, 2048], P(('rep', 'exp'), 'seq')
- key_grad: bfloat16 [32, 1024, 2048], P(('rep', 'exp'), 'seq')
- value_grad: bfloat16 [32, 1024, 2048], P(('rep', 'exp'), 'seq')
- up_grad: float32 [2, 2048, 768], P('exp', ('seq', 'rep'))
- down_grad: float32 [2, 2048, 768], P('exp', ('seq', 'rep'))
Inputs may be any that keep to these rules, and one draw needn't show every extreme that they name: `mask_pos`: the 32 entries of one device are distinct local positions of its 128. `route_rows`: for each device and expert the 128 entries are distinct local positions of that device, so each list is a permutation of the device's 128 positions (one tile of 128 rows).
All inputs are finite; a program needn't handle non-finite values.
Results may differ from a plain program's by a relative error of at most 0.018.
Values may be sent and summed in bfloat16 or wider, within the bound.
No kernel may reach another device: no remote copies, remote signals or barrier semaphores. Data moves between devices by JAX's collectives and lax.ppermute only.
A program may use at most 192 MiB of HBM per device.

v0:
```python
import jax
import jax.numpy as jnp
from jax import lax
from jax.sharding import PartitionSpec as P

HALF_HEAD_COUNT = 16
HD = 128


EPS = 1e-05


def prefix(shard, axis, combine, identity, reverse):
    devices, mine = (lax.axis_size(axis), lax.axis_index(axis))
    everything = jax.tree.map(
        lambda part, kind: lax.all_gather(part.astype(kind), axis),
        shard,
        (jnp.bfloat16, jnp.bfloat16),
    )
    start = jax.tree.map(
        lambda part, zero: jnp.broadcast_to(jnp.asarray(zero, part.dtype), part.shape),
        shard,
        identity,
    )

    def turn(k, before):
        at = devices - 1 - k if reverse else k
        reached = at > mine if reverse else at < mine
        new = combine(
            before, jax.tree.map(lambda part, own: part[at].astype(own.dtype), everything, shard)
        )
        return jax.tree.map(lambda a, b: jnp.where(reached, a, b), new, before)

    return lax.fori_loop(0, devices, turn, start)


def split_heads(matrix):
    return matrix.reshape(matrix.shape[0], HALF_HEAD_COUNT, HD).transpose(1, 0, 2)


def merge_heads(tensor):
    return tensor.transpose(1, 0, 2).reshape(tensor.shape[1], tensor.shape[0] * tensor.shape[2])


def decay_tables(cum_log):
    cum_end = cum_log[:, -1:]
    spread = jnp.exp(-jnp.abs(cum_log[:, :, None] - cum_log[:, None, :]))
    rising = jnp.exp(cum_log)
    falling = jnp.exp(cum_end - cum_log)
    endings = jnp.exp(cum_log[:, -1])
    return (spread, rising, falling, endings)


def chain(earlier, later):
    return (earlier[0] * later[0], later[0][:, None, None] * earlier[1] + later[1])


def bi_attn(query_h, key_h, value_h, tables):
    spread, rising, falling, endings = tables
    scores = jnp.einsum("hre,hse->hrs", query_h, key_h, preferred_element_type=jnp.float32)
    weights = (scores * spread).astype(jnp.bfloat16)
    inner_part = jnp.einsum("hrs,hse->hre", weights, value_h, preferred_element_type=jnp.float32)
    keys_fwd = (key_h * falling[:, :, None]).astype(jnp.bfloat16)
    keys_bwd = (key_h * rising[:, :, None]).astype(jnp.bfloat16)
    state_fwd = jnp.einsum("hse,hsf->hef", keys_fwd, value_h, preferred_element_type=jnp.float32)
    state_bwd = jnp.einsum("hse,hsf->hef", keys_bwd, value_h, preferred_element_type=jnp.float32)
    identity = (jnp.ones_like(endings), jnp.zeros_like(state_fwd))
    carried_fwd = prefix((endings, state_fwd), "seq", chain, identity, False)[1]
    carried_bwd = prefix((endings, state_bwd), "seq", chain, identity, True)[1]
    early_part = jnp.einsum(
        "hre,hef->hrf",
        query_h,
        carried_fwd.astype(jnp.bfloat16),
        preferred_element_type=jnp.float32,
    )
    late_part = jnp.einsum(
        "hre,hef->hrf",
        query_h,
        carried_bwd.astype(jnp.bfloat16),
        preferred_element_type=jnp.float32,
    )
    return inner_part + rising[:, :, None] * early_part + falling[:, :, None] * late_part


def local(
    residual_in,
    queries,
    key_feats,
    value_feats,
    log_decay,
    out_cotangent,
    mask_pos,
    route_rows,
    route_weight,
    up_proj,
    down_proj,
):
    tok_rows = queries.shape[1]
    width = queries.shape[2]
    hidden_units = up_proj.shape[2]
    cum_log = jnp.cumsum(log_decay[0], axis=1)
    tables = decay_tables(cum_log)
    query_h = split_heads(queries[0])
    key_h = split_heads(key_feats[0])
    value_h = split_heads(value_feats[0])
    rows_local = route_rows[0, 0]
    gates = route_weight[0, 0]
    token_locations = jnp.arange(tok_rows, dtype=jnp.int32)
    picks = (mask_pos[0, 0][:, None] == token_locations[None, :]).astype(jnp.bfloat16)
    out_grad = jnp.einsum(
        "mr,md->rd", picks, out_cotangent[0, 0], preferred_element_type=jnp.float32
    )
    send_grad = (gates[:, :, None] * out_grad[rows_local]).astype(jnp.bfloat16)
    attn = bi_attn(query_h, key_h, value_h, tables)
    head_scale = lax.rsqrt(jnp.mean(attn * attn, axis=-1, keepdims=True) + EPS)
    normed = attn * head_scale
    residual = (residual_in[0].astype(jnp.float32) + merge_heads(normed)).astype(jnp.bfloat16)
    residual_f = residual.astype(jnp.float32)
    row_scale = lax.rsqrt(jnp.mean(residual_f * residual_f, axis=-1, keepdims=True) + EPS)
    normalized = residual_f * row_scale
    routed = normalized.astype(jnp.bfloat16)
    rows_send = routed[rows_local]
    rows_recv, grads_recv = (
        lax.all_to_all(rows_send, "exp", split_axis=0, concat_axis=0, tiled=True),
        lax.all_to_all(send_grad, "exp", split_axis=0, concat_axis=0, tiled=True),
    )
    sources = rows_recv.shape[0]
    slots = rows_recv.shape[1]
    rows_in = rows_recv.reshape(sources * slots, width)
    grads_in = grads_recv.reshape(sources * slots, width)
    up_full, down_full = (
        lax.all_gather(up_proj, ("seq", "rep"), axis=1, tiled=True),
        lax.all_gather(down_proj, ("seq", "rep"), axis=1, tiled=True),
    )
    pre = jnp.dot(rows_in, up_full[0], preferred_element_type=jnp.float32)
    act_grad = jnp.dot(grads_in, down_full[0], preferred_element_type=jnp.float32)
    sigmoid_pre = jax.nn.sigmoid(pre)
    act = (pre * sigmoid_pre).astype(jnp.bfloat16)
    pre_grad = (act_grad * sigmoid_pre * (1.0 + pre * (1.0 - sigmoid_pre))).astype(jnp.bfloat16)
    z_part = jnp.einsum("rf,df->rd", pre_grad, up_full[0], preferred_element_type=jnp.float32)
    z_part = z_part.astype(jnp.bfloat16)
    returned = lax.all_to_all(
        z_part.reshape(sources, slots, width), "exp", split_axis=0, concat_axis=0, tiled=True
    )
    slot_hits = (rows_local[:, :, None] == token_locations[None, None, :]).astype(jnp.bfloat16)
    z_grad = jnp.einsum("ecr,ecd->rd", slot_hits, returned, preferred_element_type=jnp.float32)
    up_part = jnp.einsum("rd,rf->df", rows_in, pre_grad, preferred_element_type=jnp.float32)
    down_part = jnp.einsum("rd,rf->df", grads_in, act, preferred_element_type=jnp.float32)
    shares = lax.psum_scatter(
        jnp.concatenate((up_part, down_part), axis=1),
        ("seq", "rep"),
        scatter_dimension=0,
        tiled=True,
    )
    groups = lax.axis_size("seq") * lax.axis_size("rep")
    up_grad = (shares[:, :hidden_units] / groups)[None]
    down_grad = (shares[:, hidden_units:] / groups)[None]
    residual_grad = out_grad + row_scale * (
        z_grad - normalized * jnp.mean(z_grad * normalized, axis=-1, keepdims=True)
    )
    grad_heads = split_heads(residual_grad)
    attn_grad = (
        head_scale * (grad_heads - normed * jnp.mean(grad_heads * normed, axis=-1, keepdims=True))
    ).astype(jnp.bfloat16)
    query_part = bi_attn(attn_grad, value_h, key_h, tables)
    key_part = bi_attn(value_h, attn_grad, query_h, tables)
    value_part = bi_attn(key_h, query_h, attn_grad, tables)
    query_grad = merge_heads(query_part).astype(jnp.bfloat16)[None]
    key_grad = merge_heads(key_part).astype(jnp.bfloat16)[None]
    value_grad = merge_heads(value_part).astype(jnp.bfloat16)[None]
    return (query_grad, key_grad, value_grad, up_grad, down_grad)


def solution(mesh):
    in_specs = (
        P(("rep", "exp"), "seq", None),
        P(("rep", "exp"), "seq", None),
        P(("rep", "exp"), "seq", None),
        P(("rep", "exp"), "seq", None),
        P(("rep", "exp"), None, "seq"),
        P(("rep", "exp"), "seq", None, None),
        P(("rep", "exp"), "seq", None),
        P(("rep", "exp"), "seq", None, None),
        P(("rep", "exp"), "seq", None, None),
        P("exp", ("seq", "rep"), None),
        P("exp", ("seq", "rep"), None),
    )
    out_specs = (
        P(("rep", "exp"), "seq", None),
        P(("rep", "exp"), "seq", None),
        P(("rep", "exp"), "seq", None),
        P("exp", ("seq", "rep"), None),
        P("exp", ("seq", "rep"), None),
    )
    return jax.shard_map(local, mesh=mesh, in_specs=in_specs, out_specs=out_specs, check_vma=False)
```

profile of v0, /device:TPU:1, one launch (start us, length us, event | category | flops | bytes accessed | tf_op | source)
XLA Modules:
  0.0 1803.9 jit_solution(9896093057077340658)
XLA Ops:
  21.6 18.1 %all-reduce = bf16[128]{0:T(256)(128)(2,1)S(1)} all-reduce(bf16[128]{0:T(256)(128)(2,1)S(1)} %dynamic-update-slice), channel_id=2, replica_groups=mesh['seq'=8,'rep'=16,'exp'=2] {'seq'}, use_global_device_ids=true, to_apply=%add | all-reduce | flops 128 | bytes 512
  44.1 65.8 %all-gather.26.cloned.1.call-done = bf16[128,128,128]{2,1,0:T(8,128)(2,1)} async-done(((bf16[16,128,128]{2,1,0:T(8,128)(2,1)}), bf16[128,128,128]{2,1,0:T(8,128)(2,1)}) %all-gather.26.cloned.1.call-update) | async-done | bytes 4194320 | tf_op jit(solution)/shard_map/all_gather | solution.py:16
  109.9 20.4 %while.121 = (s32[]{:T(128)}, f32[16,128,128]{2,1,0:T(8,128)}, s32[]{:T(128)}, bf16[8,16]{1,0:T(8,128)(2,1)S(1)}, bf16[8,16,128,128]{3,2,1,0:T(8,128)(2,1)}, /*index=5*/s32[]{:T(128)}, s32[]{:T(128)}, s32[]{:T(128)}, s32[]{:T(128)}) while((s32[]{:T(128)}, f32[16,128,128]{2,1,0:T(8,128)}, s32[]{:T(128)}, ...), condition=%wide.region_4.5_spmd.clone, body=%wide.region_3.4_spmd.clone.sunk | while | flops 1310744 | bytes 2621775 | solution.py:34
  130.3 75.3 %all-gather.24.cloned.1.call-done = bf16[128,128,128]{2,1,0:T(8,128)(2,1)} async-done(((bf16[16,128,128]{2,1,0:T(8,128)(2,1)}), bf16[128,128,128]{2,1,0:T(8,128)(2,1)}) %all-gather.24.cloned.1.call-update) | async-done | bytes 4194320 | tf_op jit(solution)/shard_map/all_gather | solution.py:16
  205.6 20.1 %while.120 = (s32[]{:T(128)}, f32[16,128,128]{2,1,0:T(8,128)}, s32[]{:T(128)}, bf16[8,16]{1,0:T(8,128)(2,1)S(1)}, bf16[8,16,128,128]{3,2,1,0:T(8,128)(2,1)}, /*index=5*/s32[]{:T(128)}, s32[]{:T(128)}) while((s32[]{:T(128)}, f32[16,128,128]{2,1,0:T(8,128)}, s32[]{:T(128)}, bf16[8,16]{1,0:T(8,128)(2,1)S(1)}, ...), condition=%wide.region_2.3_spmd.clone, body=%wide.region_1.2_spmd.clone.sunk | while | flops 1310740 | bytes 2621713 | solution.py:34
  246.4 12.7 all-to-all-done.1
  263.5 158.7 %all-gather.22.cloned.1.call-done = bf16[1,2048,768]{2,1,0:T(8,128)(2,1)} async-done(((bf16[1,16,768]{2,1,0:T(8,128)(2,1)}), bf16[1,2048,768]{2,1,0:T(8,128)(2,1)}) %all-gather.22.cloned.1.call-update) | async-done | bytes 3145744 | tf_op jit(solution)/shard_map/all_gather | solution.py:132
  426.3 211.4 %all-gather.20.cloned.1.call-done = bf16[1,2048,768]{2,1,0:T(8,128)(2,1)} async-done(((bf16[1,16,768]{2,1,0:T(8,128)(2,1)}), bf16[1,2048,768]{2,1,0:T(8,128)(2,1)}) %all-gather.20.cloned.1.call-update) | async-done | bytes 3145744 | tf_op jit(solution)/shard_map/all_gather | solution.py:133
  642.4 23.5 %all_to_all.15 = bf16[2,128,2048]{2,1,0:T(8,128)(2,1)S(1)} all-to-all(bf16[2,128,2048]{2,1,0:T(8,128)(2,1)S(1)} %bitcast.309), channel_id=1, replica_groups=mesh['seq'=8,'rep'=16,'exp'=2] {'exp'}, dimensions={0} | all-to-all | bytes 2097152 | tf_op jit(solution)/shard_map/all_to_all | solution.py:142
  687.5 11.4 pad_maximum_fusion
  698.9 12.7 copy.172
  711.6 26.9 %all-gather.28.cloned.1.call-done = bf16[128,128,128]{2,1,0:T(8,128)(2,1)} async-done(((bf16[16,128,128]{2,1,0:T(8,128)(2,1)}), bf16[128,128,128]{2,1,0:T(8,128)(2,1)}) %all-gather.28.cloned.1.call-update) | async-done | bytes 4194320 | tf_op jit(solution)/shard_map/all_gather | solution.py:16
  738.5 20.2 %while.122 = (s32[]{:T(128)}, f32[16,128,128]{2,1,0:T(8,128)}, s32[]{:T(128)}, bf16[8,16]{1,0:T(8,128)(2,1)S(1)}, bf16[8,16,128,128]{3,2,1,0:T(8,128)(2,1)}, /*index=5*/s32[]{:T(128)}, s32[]{:T(128)}) while((s32[]{:T(128)}, f32[16,128,128]{2,1,0:T(8,128)}, s32[]{:T(128)}, bf16[8,16]{1,0:T(8,128)(2,1)S(1)}, ...), condition=%wide.region_10.11_spmd.clone, body=%wide.region_9.10_spmd.clone.sunk | while | flops 1310740 | bytes 2621713 | solution.py:34
  758.7 74.3 %all-gather.30.cloned.1.call-done = bf16[128,128,128]{2,1,0:T(8,128)(2,1)} async-done(((bf16[16,128,128]{2,1,0:T(8,128)(2,1)}), bf16[128,128,128]{2,1,0:T(8,128)(2,1)}) %all-gather.30.cloned.1.call-update) | async-done | bytes 4194320 | tf_op jit(solution)/shard_map/all_gather | solution.py:16
  833.0 20.1 %while.123 = (s32[]{:T(128)}, f32[16,128,128]{2,1,0:T(8,128)}, s32[]{:T(128)}, bf16[8,16]{1,0:T(8,128)(2,1)S(1)}, bf16[8,16,128,128]{3,2,1,0:T(8,128)(2,1)}, /*index=5*/s32[]{:T(128)}, s32[]{:T(128)}, s32[]{:T(128)}, s32[]{:T(128)}) while((s32[]{:T(128)}, f32[16,128,128]{2,1,0:T(8,128)}, s32[]{:T(128)}, ...), condition=%wide.region_12.13_spmd.clone, body=%wide.region_11.12_spmd.clone.sunk | while | flops 1310744 | bytes 2621775 | solution.py:34
  868.2 60.4 %all-gather.32.cloned.1.call-done = bf16[128,128,128]{2,1,0:T(8,128)(2,1)} async-done(((bf16[16,128,128]{2,1,0:T(8,128)(2,1)}), bf16[128,128,128]{2,1,0:T(8,128)(2,1)}) %all-gather.32.cloned.1.call-update) | async-done | bytes 4194320 | tf_op jit(solution)/shard_map/all_gather | solution.py:16
  928.6 20.3 %while.124 = (s32[]{:T(128)}, f32[16,128,128]{2,1,0:T(8,128)}, s32[]{:T(128)}, bf16[8,16]{1,0:T(8,128)(2,1)S(1)}, bf16[8,16,128,128]{3,2,1,0:T(8,128)(2,1)}, /*index=5*/s32[]{:T(128)}, s32[]{:T(128)}) while((s32[]{:T(128)}, f32[16,128,128]{2,1,0:T(8,128)}, s32[]{:T(128)}, bf16[8,16]{1,0:T(8,128)(2,1)S(1)}, ...), condition=%wide.region_14.15_spmd.clone, body=%wide.region_13.14_spmd.clone.sunk | while | flops 1310740 | bytes 2621713 | solution.py:34
  951.8 72.0 %all-gather.34.cloned.1.call-done = bf16[128,128,128]{2,1,0:T(8,128)(2,1)} async-done(((bf16[16,128,128]{2,1,0:T(8,128)(2,1)}), bf16[128,128,128]{2,1,0:T(8,128)(2,1)}) %all-gather.34.cloned.1.call-update) | async-done | bytes 4194320 | tf_op jit(solution)/shard_map/all_gather | solution.py:16
  1023.7 20.5 %while.125 = (s32[]{:T(128)}, f32[16,128,128]{2,1,0:T(8,128)}, s32[]{:T(128)}, bf16[8,16]{1,0:T(8,128)(2,1)S(1)}, bf16[8,16,128,128]{3,2,1,0:T(8,128)(2,1)}, /*index=5*/s32[]{:T(128)}, s32[]{:T(128)}, s32[]{:T(128)}, s32[]{:T(128)}) while((s32[]{:T(128)}, f32[16,128,128]{2,1,0:T(8,128)}, s32[]{:T(128)}, ...), condition=%wide.region_16.17_spmd.clone, body=%wide.region_15.16_spmd.clone.sunk | while | flops 1310744 | bytes 2621775 | solution.py:34
  1047.1 71.7 %all-gather.36.cloned.1.call-done = bf16[128,128,128]{2,1,0:T(8,128)(2,1)} async-done(((bf16[16,128,128]{2,1,0:T(8,128)(2,1)}), bf16[128,128,128]{2,1,0:T(8,128)(2,1)}) %all-gather.36.cloned.1.call-update) | async-done | bytes 4194320 | tf_op jit(solution)/shard_map/all_gather | solution.py:16
  1118.8 20.2 %while.126 = (s32[]{:T(128)}, f32[16,128,128]{2,1,0:T(8,128)}, s32[]{:T(128)}, bf16[8,16]{1,0:T(8,128)(2,1)S(1)}, bf16[8,16,128,128]{3,2,1,0:T(8,128)(2,1)}, /*index=5*/s32[]{:T(128)}, s32[]{:T(128)}) while((s32[]{:T(128)}, f32[16,128,128]{2,1,0:T(8,128)}, s32[]{:T(128)}, bf16[8,16]{1,0:T(8,128)(2,1)S(1)}, ...), condition=%wide.region_18.19_spmd.clone, body=%wide.region_17.18_spmd.clone.sunk | while | flops 1310740 | bytes 2621713 | solution.py:34
  1140.9 72.9 %all-gather.38.cloned.1.call-done = bf16[128,128,128]{2,1,0:T(8,128)(2,1)} async-done(((bf16[16,128,128]{2,1,0:T(8,128)(2,1)}), bf16[128,128,128]{2,1,0:T(8,128)(2,1)}) %all-gather.38.cloned.1.call-update) | async-done | bytes 4194320 | tf_op jit(solution)/shard_map/all_gather | solution.py:16
  1213.8 10.7 while.127
  1225.8 568.7 %reduce-scatter.4.cloned.1.call-done = f32[16,1536]{1,0:T(8,128)} async-done(((f32[2048,1536]{1,0:T(8,128)}), f32[16,1536]{1,0:T(8,128)}) %reduce-scatter.4.cloned.1.call-update) | async-done | bytes 98320
  (258 shorter events, 252.2 us)
Async XLA Ops:
  7.2 33.9 %copy-start = (bf16[1,1,32,2048]{3,2,1,0:T(8,128)(2,1)S(1)}, bf16[1,1,32,2048]{3,2,1,0:T(8,128)(2,1)}, u32[]{:S(2)}) copy-start(bf16[1,1,32,2048]{3,2,1,0:T(8,128)(2,1)} %param.32) | copy-start | bytes 393220
  7.2 102.7 %all-gather.26.cloned.1.call-start = ((), (), s32[]{:S(2)}) async-start(), calls=%async_computation.7 | async-start | bytes 4718592 | tf_op jit(solution)/shard_map/all_gather | solution.py:16
  11.1 6.9 copy-start.8
  12.5 193.2 %all-gather.24.cloned.1.call-start = ((), (), s32[]{:S(2)}) async-start(), calls=%async_computation.6 | async-start | bytes 4718592 | tf_op jit(solution)/shard_map/all_gather | solution.py:16
  13.8 6.3 copy-start.14
  13.8 26.1 %copy-start.6 = (bf16[1,128,2048]{2,1,0:T(8,128)(2,1)S(1)}, bf16[1,128,2048]{2,1,0:T(8,128)(2,1)}, u32[]{:S(2)}) copy-start(bf16[1,128,2048]{2,1,0:T(8,128)(2,1)} %param.27) | copy-start | bytes 1572868
  13.8 408.4 %all-gather.22.cloned.1.call-start = ((), (), s32[]{:S(2)}) async-start(), calls=%async_computation.5 | async-start | bytes 3170304 | tf_op jit(solution)/shard_map/all_gather | solution.py:132
  14.5 623.2 %all-gather.20.cloned.1.call-start = ((), (), s32[]{:S(2)}) async-start(), calls=%async_computation.4 | async-start | bytes 3170304 | tf_op jit(solution)/shard_map/all_gather | solution.py:133
  15.1 723.4 %all-gather.28.cloned.1.call-start = ((), (), s32[]{:S(2)}) async-start(), calls=%async_computation.8 | async-start | bytes 4718592 | tf_op jit(solution)/shard_map/all_gather | solution.py:16
  16.4 24.6 %copy-start.10 = (s32[1,1,2,128]{3,2,1,0:T(2,128)S(1)}, s32[1,1,2,128]{3,2,1,0:T(2,128)}, u32[]{:S(2)}) copy-start(s32[1,1,2,128]{3,2,1,0:T(2,128)} %param.34) | copy-start | bytes 3076
  16.4 24.6 %copy-start.12 = (s32[1,1,32]{2,1,0:T(1,128)S(1)}, s32[1,1,32]{2,1,0:T(1,128)}, u32[]{:S(2)}) copy-start(s32[1,1,32]{2,1,0:T(1,128)} %param.33) | copy-start | bytes 388
  16.5 816.5 %all-gather.30.cloned.1.call-start = ((), (), s32[]{:S(2)}) async-start(), calls=%async_computation.9 | async-start | bytes 4718592 | tf_op jit(solution)/shard_map/all_gather | solution.py:16
  236.9 6.8 copy-start.11
  239.2 19.9 %all-to-all-start.1 = ((bf16[2,128,2048]{2,1,0:T(8,128)(2,1)}), bf16[2,128,2048]{2,1,0:T(8,128)(2,1)}, u32[]{:S(2)}, u32[]{:S(2)}) async-start(bf16[2,128,2048]{2,1,0:T(8,128)(2,1)} %bitcast.295), calls=%async_computation.1 | async-start | bytes 2097152 | tf_op jit(solution)/shard_map/all_to_all | solution.py:124
  259.1 167.3 %all-to-all-start = ((bf16[2,128,2048]{2,1,0:T(8,128)(2,1)}), bf16[2,128,2048]{2,1,0:T(8,128)(2,1)}, u32[]{:S(2)}, u32[]{:S(2)}) async-start(bf16[2,128,2048]{2,1,0:T(8,128)(2,1)} %multiply_convert_fusion), calls=%async_computation | async-start | bytes 2097152 | tf_op jit(solution)/shard_map/all_to_all | solution.py:125
  263.5 665.1 %all-gather.32.cloned.1.call-start = ((), (), s32[]{:S(2)}) async-start(), calls=%async_computation.10 | async-start | bytes 4718592 | tf_op jit(solution)/shard_map/all_gather | solution.py:16
  641.3 24.9 %copy-start.9 = (bf16[256,768]{1,0:T(8,128)(2,1)}, bf16[256,768]{1,0:T(8,128)(2,1)S(1)}, u32[]{:S(2)}) copy-start(bf16[256,768]{1,0:T(8,128)(2,1)S(1)} %fusion.40) | copy-start | bytes 1179652
  641.3 24.5 %copy-start.4 = (bf16[128,2048]{1,0:T(8,128)(2,1)S(1)}, bf16[128,2048]{1,0:T(8,128)(2,1)}, u32[]{:S(2)}) copy-start(bf16[128,2048]{1,0:T(8,128)(2,1)} %get-tuple-element.1157) | copy-start | bytes 1572868
  673.3 350.4 %all-gather.34.cloned.1.call-start = ((), (), s32[]{:S(2)}) async-start(), calls=%async_computation.11 | async-start | bytes 4718592 | tf_op jit(solution)/shard_map/all_gather | solution.py:16
  674.7 444.2 %all-gather.36.cloned.1.call-start = ((), (), s32[]{:S(2)}) async-start(), calls=%async_computation.12 | async-start | bytes 4718592 | tf_op jit(solution)/shard_map/all_gather | solution.py:16
  676.0 537.8 %all-gather.38.cloned.1.call-start = ((), (), s32[]{:S(2)}) async-start(), calls=%async_computation.13 | async-start | bytes 4718592 | tf_op jit(solution)/shard_map/all_gather | solution.py:16
  677.4 5.1 copy-start.7
  677.4 1117.2 %reduce-scatter.4.cloned.1.call-start = ((), (), s32[]{:S(2)}) async-start(), calls=%async_computation.14 | async-start | bytes 12681216
  1224.5 572.9 %copy-start.1 = (bf16[1,1,32,2048]{3,2,1,0:T(8,128)(2,1)S(1)}, bf16[1,1,32,2048]{3,2,1,0:T(8,128)(2,1)}, u32[]{:S(2)}) copy-start(bf16[1,1,32,2048]{3,2,1,0:T(8,128)(2,1)} %param.32) | copy-start | bytes 393220
  (4 other events, 16.7 us)
Sparse Core Ops, SparseCore 0:
  12.6 97.2 all-gather.25
  112.3 93.3 all-gather.23
  207.5 214.6 all-gather.21
  424.0 213.6 all-gather.19
  639.9 98.5 all-gather.27
  740.1 92.7 all-gather.29
  835.3 93.2 all-gather.31
  930.4 93.2 all-gather.33
  1025.5 93.2 all-gather.35
  1120.5 93.2 all-gather.37
  1216.3 578.2 reduce-scatter.3
where the time goes:
time: 1810 us; the launch traced here: 1800 us
  waiting for transfers between devices  1470 us (81%)
  other arithmetic  175 us (10%)
  matrix products  53.8 us (3%)
  blocking collectives  41.6 us (2%)
  local copies, waits for them, and re-layouts  36.3 us (2%)
    unnamed x12, waiting for transfers between devices  570 us
    all_gather x8, waiting for transfers between devices, prefix(): lax.all_gather(part.astype(kind), axis)  519 us
    all_gather x1, waiting for transfers between devices, local(): lax.all_gather(down_proj, ('seq', 'rep'), axis=1, tiled=True)  211 us
    all_gather x1, waiting for transfers between devices, local(): lax.all_gather(up_proj, ('seq', 'rep'), axis=1, tiled=True)  159 us
    select_n x64, other arithmetic, turn(): return jax.tree.map(lambda a, b: jnp.where(reached, a, b), new, before)  152 us
  transfers between devices with their start and end apart: 13, of which 12 were waited for; matrix products, arithmetic and copies ran while one was open for 14% of the time, Pallas kernels for 0%

commit v1 on v0

v1 whole, which is shorter than its diff:
```python
import jax
import jax.numpy as jnp
from jax import lax
from jax.experimental import pallas as pl
from jax.experimental.pallas import tpu as pltpu
from jax.sharding import Mesh, PartitionSpec as P

HEADS = 16
HD = 128
EPS = 1e-05
SEQ = ("y", "xl")
GRP = ("xl", "c", "e")
F32 = jnp.float32
BF16 = jnp.bfloat16
HIGH = lax.Precision.HIGHEST


def call(body, outs, *args, flops=10**8, scalar=False):
    shapes = [jax.ShapeDtypeStruct(s, d) for s, d in outs]
    moved = sum(a.size * a.dtype.itemsize for a in (*args, *shapes))
    spaces = [pltpu.SMEM if scalar and k == 0 else pltpu.VMEM for k in range(len(args))]
    result = pl.pallas_call(
        body,
        out_shape=shapes,
        in_specs=[pl.BlockSpec(memory_space=m) for m in spaces],
        compiler_params=pltpu.CompilerParams(vmem_limit_bytes=44 << 20),
        cost_estimate=pl.CostEstimate(flops=flops, bytes_accessed=moved, transcendentals=0),
    )(*args)
    return result


def iota(shape, dim):
    return lax.broadcasted_iota(jnp.int32, shape, dim)


def tn(a, b, **kw):
    return lax.dot_general(a, b, (((0,), (0,)), ((), ())), preferred_element_type=F32, **kw)


def nt(a, b, **kw):
    return lax.dot_general(a, b, (((1,), (1,)), ((), ())), preferred_element_type=F32, **kw)


def nn(a, b, **kw):
    return lax.dot_general(a, b, (((1,), (0,)), ((), ())), preferred_element_type=F32, **kw)


def head(h):
    return slice(h * HD, (h + 1) * HD)


def exchange(x, axes):
    return lax.all_to_all(x, axes, split_axis=0, concat_axis=0, tiled=True)


def broadcast(x, axes, n):
    return exchange(jnp.broadcast_to(x[None], (n, *x.shape)), axes)


def weights_body(up, down, out):
    low = iota((up.shape[0], HD), 1) < 64
    for c in range(12):
        u = up[:, head(c // 2)].astype(F32)
        d = down[:, head(c // 2)].astype(F32)
        if c % 2:
            u = pltpu.roll(u, 64, 1)
        else:
            d = pltpu.roll(d, 64, 1)
        out[c // 3, :, head(c % 3)] = jnp.where(low, u, d).astype(BF16)


def weight_grads_body(scale, g, up, down):
    low = iota((up.shape[0], HD), 1) < 64
    for b in range(6):
        first, second = 2 * b, 2 * b + 1
        x = g[first // 3, :, head(first % 3)] * scale
        y = g[second // 3, :, head(second % 3)] * scale
        up[:, head(b)] = jnp.where(low, x, pltpu.roll(y, 64, 1))
        down[:, head(b)] = jnp.where(low, pltpu.roll(x, 64, 1), y)


def states_body(ld, key, value, places, out, cum_out, cum_t_out):
    rows, cols = iota((HD, HD), 0), iota((HD, HD), 1)
    ldv = ld[...]
    cum = nn(ldv, (rows <= cols).astype(F32), precision=HIGH)
    cum_t = nt((cols <= rows).astype(F32), ldv, precision=HIGH)
    cum_out[...] = cum
    cum_t_out[...] = cum_t
    falling = jnp.exp(cum_t[HD - 1 : HD, :] - cum_t)
    rising = jnp.exp(cum_t)
    for h in range(HEADS):
        k = key[:, head(h)].astype(F32)
        kf = (k * falling[:, h : h + 1]).astype(BF16)
        kb = (k * rising[:, h : h + 1]).astype(BF16)
        v = value[:, head(h)]
        g, at = h // 2, (h % 2) * HD
        out[g, at : at + HD, :] = tn(kf, v).astype(BF16)
        out[g, 256 + at : 256 + at + HD, :] = tn(kb, v).astype(BF16)
    chosen = nn(cum, (rows == places[...]).astype(F32), precision=HIGH)
    hi = chosen.astype(BF16).astype(F32)
    mid = (chosen - hi).astype(BF16).astype(F32)
    low = (chosen - hi - mid).astype(BF16).astype(F32)
    lane = iota((HEADS, HD), 1)
    first = (lane < 32) | (lane == 96)
    second = ((lane >= 32) & (lane < 64)) | (lane == 97)
    third = ((lane >= 64) & (lane < 96)) | (lane == 98)
    packed = jnp.where(first, hi, jnp.where(second, mid, jnp.where(third, low, 0.0))).astype(BF16)
    for g in range(8):
        out[g, 512:528, :] = packed


def masked_body(
    query, key, value, residual, cot, mask, routes, gates, cum, cum_t, qm_out, rm_out, inner_out, sg_out, cm_out
):
    pick_t = (iota((HD, 32), 0) == mask[...]).astype(BF16)
    qm = tn(pick_t, query[...]).astype(BF16)
    qm_out[...] = qm
    rm_out[...] = tn(pick_t, residual[...])
    lane = iota((HD, HD), 1)
    sub = iota((HD, HD), 0)
    pick_f = pick_t.astype(F32)
    cm = tn(pick_f, cum_t[...], precision=HIGH)
    cm_out[...] = cm
    cumv = cum[...]
    for h in range(HEADS):
        s = nt(qm[:, head(h)], key[:, head(h)])
        p = (s * jnp.exp(-jnp.abs(cm[:, h : h + 1] - cumv[h : h + 1, :]))).astype(BF16)
        inner_out[:, head(h)] = nn(p, value[:, head(h)])
    table = jnp.zeros((HD, HD), F32)
    for e in range(2):
        hit = jnp.where(sub == routes[e : e + 1, :], gates[e : e + 1, :], 0.0)
        table = jnp.where(lane == e, jnp.sum(hit, axis=1, keepdims=True), table)
    gm = tn(pick_f, table, precision=HIGH)
    cotf = cot[...].astype(F32)
    for e in range(2):
        sg = (gm[:, e : e + 1] * cotf).astype(BF16)
        for k in range(4):
            sg_out[2 * k + e] = sg


def carry_body(mine, parts, out):
    row, lane = iota((HEADS, HD), 0), iota((HEADS, HD), 1)
    ends = (lane >= 96) & (lane < 99)
    n = parts.shape[0]
    for j in range(2):
        at = slice(j * HD, (j + 1) * HD)
        back = slice(256 + j * HD, 256 + (j + 1) * HD)
        wanted = ends & (row == 2 * mine[0] + j)
        decay = [
            jnp.exp(jnp.sum(jnp.where(wanted, parts[a, 512:528, :].astype(F32), 0.0), keepdims=True))
            for a in range(n)
        ]
        run = jnp.zeros((HD, HD), F32)
        for a in range(n):
            out[a, at, :] = run.astype(BF16)
            run = decay[a] * run + parts[a, at, :].astype(F32)
        run = jnp.zeros((HD, HD), F32)
        for a in reversed(range(n)):
            out[a, back, :] = run.astype(BF16)
            run = decay[a] * run + parts[a, back, :].astype(F32)


def states_of(carried, h):
    at = (h % 2) * HD
    return carried[h // 2, at : at + HD, :], carried[h // 2, 256 + at : 256 + at + HD, :]


def rows_body(qm, rm, inner, cm, cum_t, carried, routed_out, normed_out, normalized_out, stats_out):
    cmv = cm[...]
    rising = jnp.exp(cmv)
    falling = jnp.exp(cum_t[HD - 1 : HD, :] - cmv)
    lane = iota((32, HD), 1)
    stats = jnp.zeros((32, HD), F32)
    total = jnp.zeros((32, HD), F32)
    residuals = []
    for h in range(HEADS):
        fwd, bwd = states_of(carried, h)
        q = qm[:, head(h)]
        attn = inner[:, head(h)] + rising[:, h : h + 1] * nn(q, fwd) + falling[:, h : h + 1] * nn(q, bwd)
        scale = lax.rsqrt(jnp.mean(attn * attn, axis=-1, keepdims=True) + EPS)
        normed = attn * scale
        normed_out[:, head(h)] = normed
        stats = jnp.where(lane == h, scale, stats)
        r = (rm[:, head(h)] + normed).astype(BF16).astype(F32)
        total = total + r * r
        residuals.append(r)
    row_scale = lax.rsqrt(jnp.sum(total, axis=-1, keepdims=True) * (1.0 / (HEADS * HD)) + EPS)
    stats_out[...] = jnp.where(lane == HEADS, row_scale, stats)
    for h in range(HEADS):
        normalized = residuals[h] * row_scale
        normalized_out[:, head(h)] = normalized
        routed = normalized.astype(BF16)
        for k in range(8):
            routed_out[k, :, head(h)] = routed


def expert_body(rows, grads, weights, z_out, dw_out, w_ref):
    ny, nz, nx, unit = weights.shape[:4]
    for y in range(ny):
        for z in range(nz):
            for x in range(nx):
                w_ref[pl.ds(((y * nx + x) * nz + z) * unit, unit), :] = weights[y, z, x]
    r = rows[...].reshape(256, HEADS * HD)
    g = grads[...].reshape(256, HEADS * HD)
    w = w_ref[...]
    pre_all = nn(r, w)
    grad_all = nn(g, w)
    low = iota((256, HD), 1) < 64
    pgs, acts = [], []
    for b in range(3):
        pre = pre_all[:, head(b)]
        act_grad = pltpu.roll(grad_all[:, head(b)], 64, 1)
        sig = jax.nn.sigmoid(pre)
        act = pltpu.roll(pre * sig, 64, 1)
        pre_grad = act_grad * sig * (1.0 + pre * (1.0 - sig))
        pgs.append(jnp.where(low, pre_grad, 0.0).astype(BF16))
        acts.append(jnp.where(low, 0.0, act).astype(BF16))
    pg = jnp.concatenate(pgs, axis=1)
    ac = jnp.concatenate(acts, axis=1)
    z_out[...] = nt(pg, w).astype(BF16).reshape(z_out.shape)
    both = jnp.concatenate((pg, ac), axis=0)
    for y in range(4):
        cols = slice(y * 512, (y + 1) * 512)
        sides = jnp.concatenate((r[:, cols], g[:, cols]), axis=0)
        dw_out[y] = tn(sides, both).astype(BF16)


def sum_y_body(parts, out):
    ny = parts.shape[0]
    nz, nx, unit = out.shape[:3]
    for x in range(nx):
        for z in range(nz):
            at = slice((x * nz + z) * unit, (x * nz + z + 1) * unit)
            total = parts[0, at, :].astype(F32)
            for y in range(1, ny):
                total = total + parts[y, at, :].astype(F32)
            out[z, x] = total.astype(BF16)


def sum_z_body(parts, out):
    total = parts[0].astype(F32)
    for z in range(1, parts.shape[0]):
        total = total + parts[z].astype(F32)
    out[...] = total


def grads_body(z_parts, cot, normed, normalized, stats, out):
    z = z_parts[0].astype(F32)
    for k in range(1, 8):
        z = z + z_parts[k].astype(F32)
    norm = normalized[...]
    st = stats[...]
    mean = jnp.sum(z * norm, axis=-1, keepdims=True) * (1.0 / (HEADS * HD))
    rg = cot[...].astype(F32) + st[:, HEADS : HEADS + 1] * (z - norm * mean)
    for h in range(HEADS):
        n = normed[:, head(h)]
        g = rg[:, head(h)]
        m = jnp.mean(g * n, axis=-1, keepdims=True)
        a = (st[:, h : h + 1] * (g - n * m)).astype(BF16)
        for k in range(8):
            out[k, :, head(h)] = a


def query_grad_body(da8, key, value, mask, cm, cum, cum_t, carried, out):
    da = da8[0]
    pick_t = (iota((HD, 32), 0) == mask[...]).astype(BF16)
    cmv = cm[...]
    cumv = cum[...]
    rising = jnp.exp(cmv)
    falling = jnp.exp(cum_t[HD - 1 : HD, :] - cmv)
    for h in range(HEADS):
        fwd, bwd = states_of(carried, h)
        a = da[:, head(h)]
        s = nt(a, value[:, head(h)])
        p = (s * jnp.exp(-jnp.abs(cmv[:, h : h + 1] - cumv[h : h + 1, :]))).astype(BF16)
        q = nn(p, key[:, head(h)]) + rising[:, h : h + 1] * nt(a, fwd) + falling[:, h : h + 1] * nt(a, bwd)
        out[:, head(h)] = nn(pick_t, q.astype(BF16)).astype(BF16)


def scores_body(mine, parts, qm_all, key, cum_t, decay_out, scores_out):
    n = parts.shape[0]
    lane, col = iota((HD, n * 32), 0), iota((HD, n * 32), 1)
    block = col // 32
    me = mine[0]
    at = jnp.zeros((HEADS, n * 32), F32)
    for a in range(n):
        own = (lane < 96) & (lane % 32 == col % 32) & (block == a)
        ends = (lane >= 96) & (lane < 99)
        after = ends & (block > a) & (a >= me)
        before = ends & (block <= a) & (a < me)
        take = jnp.where(own | after, 1.0, jnp.where(before, -1.0, 0.0)).astype(BF16)
        at = at + nn(parts[a, 512:528, :], take)
    ct = cum_t[...]
    for h in range(HEADS):
        decay = jnp.exp(-jnp.abs(ct[:, h : h + 1] - at[h : h + 1, :]))
        decay_out[h] = decay
        qm = qm_all[:, :, head(h)].reshape(n * 32, HD)
        scores_out[h] = (nt(key[:, head(h)], qm) * decay).astype(BF16)


def key_value_grads_body(da_all, qm_all, value, decay, scores, key_out, value_out):
    rows = da_all.shape[0] * 32
    for h in range(HEADS):
        da = da_all[:, :, head(h)].reshape(rows, HD)
        qm = qm_all[:, :, head(h)].reshape(rows, HD)
        value_out[:, head(h)] = nn(scores[h], da).astype(BF16)
        p = (nt(value[:, head(h)], da) * decay[h]).astype(BF16)
        key_out[:, head(h)] = nn(p, qm).astype(BF16)


def local(residual, query, key, value, ld, cot, mask, routes, gates, up, down):
    residual, query, key, value, ld = residual[0], query[0], key[0], value[0], ld[0]
    cot, mask, routes, gates, up, down = cot[0, 0], mask[0], routes[0, 0], gates[0, 0], up[0], down[0]
    width = HEADS * HD
    ny, nx, nz, nc = (lax.axis_size(a) for a in ("y", "xl", "z", "c"))
    shard = up.shape[0]
    mine = (lax.axis_index("y") * nx + lax.axis_index("xl")).astype(jnp.int32).reshape(1)
    places = jnp.concatenate((mask, mask, mask, jnp.full_like(mask, HD - 1)), axis=1)

    [w0] = call(weights_body, [((4, shard, 384), BF16)], up, down)
    states, cum, cum_t = call(
        states_body,
        [((8, 528, HD), BF16), ((HEADS, HD), F32), ((HD, HEADS), F32)],
        ld, key, value, places,
    )
    parts = exchange(states, SEQ)
    w1 = exchange(w0, ("xl", "c"))
    qm, rm, inner, sg, cm = call(
        masked_body,
        [((32, width), BF16), ((32, width), F32), ((32, width), F32), ((8, 32, width), BF16), ((32, HEADS), F32)],
        query, key, value, residual, cot, mask, routes, gates, cum, cum_t,
    )
    [carries] = call(carry_body, [((8, 512, HD), BF16)], mine, parts, scalar=True)
    carried = exchange(carries, SEQ)
    w2 = broadcast(w1.reshape(4 * shard, 384), "z", nz)
    w3 = broadcast(w2.reshape(nz * 4 * shard, 384), "y", ny)
    grads = exchange(sg, GRP)
    routed8, normed, normalized, stats = call(
        rows_body,
        [((8, 32, width), BF16), ((32, width), F32), ((32, width), F32), ((32, HD), F32)],
        qm, rm, inner, cm, cum_t, carried,
    )
    rows = exchange(routed8, GRP)
    weights = w3.reshape(ny, nz, nx, nc * shard, 384)
    z_send, dw = expert_call(rows, grads, weights, ny)
    z_parts = exchange(z_send, GRP)
    [da8] = call(grads_body, [((8, 32, width), BF16)], z_parts, cot, normed, normalized, stats)
    da_all = exchange(da8, SEQ)
    qm_all = broadcast(qm, SEQ, 8)
    [query_grad] = call(query_grad_body, [((HD, width), BF16)], da8, key, value, mask, cm, cum, cum_t, carried)
    decay, scores = call(
        scores_body,
        [((HEADS, HD, 256), F32), ((HEADS, HD, 256), BF16)],
        mine, parts, qm_all, key, cum_t,
        scalar=True,
    )
    key_grad, value_grad = call(
        key_value_grads_body,
        [((HD, width), BF16), ((HD, width), BF16)],
        da_all, qm_all, value, decay, scores,
    )
    d1 = exchange(dw, "y")
    [d2] = call(sum_y_body, [((nz, nx, nc * shard, 384), BF16)], d1)
    d3 = exchange(d2, "z")
    [d4] = call(sum_z_body, [((nx, nc * shard, 384), F32)], d3)
    d5 = exchange(d4.reshape(4, shard, 384), ("xl", "c"))
    scale = 1.0 / (ny * nx * nz * nc)

    def finish(g, a, b):
        weight_grads_body(scale, g, a, b)

    up_grad, down_grad = call(finish, [((shard, 768), F32), ((shard, 768), F32)], d5)
    return query_grad[None], key_grad[None], value_grad[None], up_grad[None], down_grad[None]


def expert_call(rows, grads, weights, ny):
    width = rows.shape[2]
    outs = [
        jax.ShapeDtypeStruct(rows.shape, BF16),
        jax.ShapeDtypeStruct((ny, width // ny, 384), BF16),
    ]
    moved = sum(a.size * a.dtype.itemsize for a in (rows, grads, weights, *outs))
    return pl.pallas_call(
        expert_body,
        out_shape=outs,
        scratch_shapes=[pltpu.VMEM((width, 384), BF16)],
        compiler_params=pltpu.CompilerParams(vmem_limit_bytes=44 << 20),
        cost_estimate=pl.CostEstimate(flops=2 * 10**9, bytes_accessed=moved, transcendentals=0),
    )(rows, grads, weights)


def solution(mesh):
    shape = mesh.shape
    grid = mesh.devices.reshape(shape["seq"] // 2, 2, shape["rep"] // 2, 2, shape["exp"])
    fine = Mesh(grid, ("y", "xl", "z", "c", "e"))
    sequences, data = ("z", "c", "e"), ("y", "xl", "z", "c")
    in_specs = (
        P(sequences, SEQ, None),
        P(sequences, SEQ, None),
        P(sequences, SEQ, None),
        P(sequences, SEQ, None),
        P(sequences, None, SEQ),
        P(sequences, SEQ, None, None),
        P(sequences, SEQ, None),
        P(sequences, SEQ, None, None),
        P(sequences, SEQ, None, None),
        P("e", data, None),
        P("e", data, None),
    )
    out_specs = (
        P(sequences, SEQ, None),
        P(sequences, SEQ, None),
        P(sequences, SEQ, None),
        P("e", data, None),
        P("e", data, None),
    )
    return jax.shard_map(local, mesh=fine, in_specs=in_specs, out_specs=out_specs, check_vma=False)
```

time: 1810 us -> 262 us (0.14)
  waiting for transfers between devices: 1470 us -> 91.9 us
  other arithmetic: 175 us -> 0.08 us
  matrix products: 53.8 us -> 0 us
  starting transfers between devices: 9.28 us -> 45.1 us
  blocking collectives: 41.6 us -> 71.1 us
  Pallas kernels: 0 us -> 29.2 us
    all_gather x10 -> x0, waiting for transfers between devices: 889 us -> none  [the longest x8 519 us: prefix(): lax.all_gather(part.astype(kind), axis)]
    unnamed x12 -> x0, waiting for transfers between devices: 570 us -> none
    select_n x65 -> x0, other arithmetic: 152 us -> none  [the longest x64 152 us: turn(): return jax.tree.map(lambda a, b: jnp.where(reached, a, b), new, before)]
    all_to_all x2 -> x9, waiting for transfers between devices: 12.7 us -> 91.9 us  [exchange(): return lax.all_to_all(x, axes, split_axis=0, concat_axis=0, tiled=True)]
    dot_general x28 -> x0, matrix products: 53.8 us -> none  [the longest x4 8.22 us: bi_attn(): jnp.einsum('hrs,hse->hre', weights, value_h, preferred_element_type=jnp.f...]
    all_to_all x1 -> x4, blocking collectives: 23.5 us -> 71.1 us  [exchange(): return lax.all_to_all(x, axes, split_axis=0, concat_axis=0, tiled=True)]
    all_to_all x2 -> x9, starting transfers between devices: 8.84 us -> 45.1 us  [exchange(): return lax.all_to_all(x, axes, split_axis=0, concat_axis=0, tiled=True)]
    pallas_call x0 -> x13, Pallas kernels: none -> 29.2 us  [the longest x12 24.8 us: call(): pl.pallas_call(body, out_shape=shapes, in_specs=[pl.BlockSpec(memory_spac...]
  transfers between devices with their start and end apart: 13 -> 9, of which waited for: 12 -> 8; matrix products, arithmetic and copies ran while one was open for 14% -> 0% of each run, Pallas kernels for 0% -> 11%
where the time goes in v1:
time: 262 us; the launch traced here: 261 us
  waiting for transfers between devices  91.9 us (35%)
  blocking collectives  71.1 us (27%)
  starting transfers between devices  45.1 us (17%)
  Pallas kernels  29.2 us (11%)
  local copies, waits for them, and re-layouts  22.6 us (9%)
    all_to_all x9, waiting for transfers between devices, exchange(): return lax.all_to_all(x, axes, split_axis=0, concat_axis=0, tiled=True)  91.9 us
    all_to_all x4, blocking collectives, exchange(): return lax.all_to_all(x, axes, split_axis=0, concat_axis=0, tiled=True)  71.1 us
    all_to_all x9, starting transfers between devices, exchange(): return lax.all_to_all(x, axes, split_axis=0, concat_axis=0, tiled=True)  45.1 us
    pallas_call x12, Pallas kernels, call(): pl.pallas_call(body, out_shape=shapes, in_specs=[pl.BlockSpec(memory_spac...  24.8 us
    unnamed x60, local copies, waits for them, and re-layouts  18.5 us
  transfers between devices with their start and end apart: 9, of which 8 were waited for; matrix products, arithmetic and copies ran while one was open for 0% of the time, Pallas kernels for 11%

profile of v1, /device:TPU:1, one launch (start us, length us, event | category | flops | bytes accessed | tf_op | source)
XLA Modules:
  0.0 260.8 jit_solution(695101623146323613)
XLA Ops:
  2.3 8.8 %all_to_all.65 = bf16[4,16,384]{2,1,0:T(8,128)(2,1)S(1)} all-to-all(bf16[4,16,384]{2,1,0:T(8,128)(2,1)S(1)} %shard_map.150), channel_id=1, replica_groups=mesh['y'=4,'xl'=2,'z'=8,'c'=2,'e'=2] {'xl','c'}, dimensions={0} | all-to-all | bytes 98304 | tf_op jit(solution)/shard_map/all_to_all | solution.py:53
  11.9 6.7 %all-to-all-start.5 = ((bf16[8,64,384]{2,1,0:T(8,128)(2,1)}), bf16[8,64,384]{2,1,0:T(8,128)(2,1)}, u32[]{:S(2)}, u32[]{:S(2)}) async-start(bf16[8,64,384]{2,1,0:T(8,128)(2,1)} %broadcast_in_dim.40), calls=%async_computation.5 | async-start | bytes 786432 | tf_op jit(solution)/shard_map/all_to_all | solution.py:53
  21.7 10.6 %all-to-all-done.5 = bf16[8,64,384]{2,1,0:T(8,128)(2,1)} async-done(((bf16[8,64,384]{2,1,0:T(8,128)(2,1)}), bf16[8,64,384]{2,1,0:T(8,128)(2,1)}, u32[]{:S(2)}, u32[]{:S(2)}) %all-to-all-start.5) | async-done | bytes 393248 | tf_op jit(solution)/shard_map/all_to_all | solution.py:53
  32.2 4.2 %all-to-all-start = ((bf16[8,528,128]{2,1,0:T(8,128)(2,1)}), bf16[8,528,128]{2,1,0:T(8,128)(2,1)S(1)}, u32[]{:S(2)}, u32[]{:S(2)}) async-start(bf16[8,528,128]{2,1,0:T(8,128)(2,1)} %get-tuple-element.31), calls=%async_computation | async-start | bytes 2162688 | tf_op jit(solution)/shard_map/all_to_all | solution.py:53
  36.5 4.1 %shard_map.147 = (bf16[32,2048]{1,0:T(8,128)(2,1)S(1)}, f32[32,2048]{1,0:T(8,128)S(1)}, f32[32,2048]{1,0:T(8,128)S(1)}, bf16[8,32,2048]{2,1,0:T(8,128)(2,1)}, f32[32,16]{1,0:T(8,128)S(1)}) custom-call(bf16[128,2048]{1,0:T(8,128)(2,1)S(1)} %bitcast.31, bf16[128,2048]{1,0:T(8,128)(2,1)S(1)} %bitcast.24, bf16[128,2048]{1,0:T(8,128)(2,1)S(1)} %bitcast.28, ...), custom_call_target="tpu_custom_call" | custom-call | flops 100000000 | bytes 3952768 | tf_op jit(solution)/shard_map/pallas_call | solution.py:22
  42.0 8.3 %all-to-all-done.parts = bf16[8,528,128]{2,1,0:T(8,128)(2,1)S(1)} async-done(((bf16[8,528,128]{2,1,0:T(8,128)(2,1)}), bf16[8,528,128]{2,1,0:T(8,128)(2,1)S(1)}, u32[]{:S(2)}, u32[]{:S(2)}) %all-to-all-start) | async-done | bytes 1081376 | tf_op jit(solution)/shard_map/all_to_all | solution.py:53
  50.2 7.3 %all-to-all-start.3 = ((bf16[8,32,2048]{2,1,0:T(8,128)(2,1)}), bf16[8,32,2048]{2,1,0:T(8,128)(2,1)S(1)}, u32[]{:S(2)}, u32[]{:S(2)}) async-start(bf16[8,32,2048]{2,1,0:T(8,128)(2,1)} %get-tuple-element.33), calls=%async_computation.3 | async-start | bytes 2097152 | tf_op jit(solution)/shard_map/all_to_all | solution.py:53
  57.9 14.6 %all-to-all-done.3.grads = bf16[8,32,2048]{2,1,0:T(8,128)(2,1)S(1)} async-done(((bf16[8,32,2048]{2,1,0:T(8,128)(2,1)}), bf16[8,32,2048]{2,1,0:T(8,128)(2,1)S(1)}, u32[]{:S(2)}, u32[]{:S(2)}) %all-to-all-start.3) | async-done | bytes 1048608 | tf_op jit(solution)/shard_map/all_to_all | solution.py:53
  73.5 17.9 %all_to_all.66.carried = bf16[8,512,128]{2,1,0:T(8,128)(2,1)S(1)} all-to-all(bf16[8,512,128]{2,1,0:T(8,128)(2,1)S(1)} %shard_map.148), channel_id=1, replica_groups=mesh['y'=4,'xl'=2,'z'=8,'c'=2,'e'=2] {'y','xl'}, dimensions={0} | all-to-all | bytes 2097152 | tf_op jit(solution)/shard_map/all_to_all | solution.py:53
  93.7 4.4 %all-to-all-start.6 = ((bf16[4,512,384]{2,1,0:T(8,128)(2,1)}), bf16[4,512,384]{2,1,0:T(8,128)(2,1)}, u32[]{:S(2)}, u32[]{:S(2)}) async-start(bf16[4,512,384]{2,1,0:T(8,128)(2,1)} %broadcast_in_dim.42), calls=%async_computation.6 | async-start | bytes 3145728 | tf_op jit(solution)/shard_map/all_to_all | solution.py:53
  102.7 15.0 %all-to-all-done.6 = bf16[4,512,384]{2,1,0:T(8,128)(2,1)} async-done(((bf16[4,512,384]{2,1,0:T(8,128)(2,1)}), bf16[4,512,384]{2,1,0:T(8,128)(2,1)}, u32[]{:S(2)}, u32[]{:S(2)}) %all-to-all-start.6) | async-done | bytes 1572896 | tf_op jit(solution)/shard_map/all_to_all | solution.py:53
  117.7 20.2 %all_to_all.67.rows = bf16[8,32,2048]{2,1,0:T(8,128)(2,1)} all-to-all(bf16[8,32,2048]{2,1,0:T(8,128)(2,1)S(1)} %get-tuple-element.32), channel_id=1, replica_groups=mesh['y'=4,'xl'=2,'z'=8,'c'=2,'e'=2] {'xl','c','e'}, dimensions={0} | all-to-all | bytes 2097152 | tf_op jit(solution)/shard_map/all_to_all | solution.py:53
  145.0 4.5 %shard_map.151 = (bf16[8,32,2048]{2,1,0:T(8,128)(2,1)S(1)}, bf16[4,512,384]{2,1,0:T(8,128)(2,1)S(1)}) custom-call(bf16[8,32,2048]{2,1,0:T(8,128)(2,1)S(1)} %copy-done.12, bf16[8,32,2048]{2,1,0:T(8,128)(2,1)S(1)} %copy-done.10, bf16[4,8,2,32,384]{4,3,2,1,0:T(8,128)(2,1)} %bitcast.14.weights), custom_call_target="tpu_custom_call" | custom-call | flops 2000000000 | bytes 6291456 | tf_op jit(solution)/shard_map/pallas_call | solution.py:383
  151.6 6.8 %all-to-all-done.9.qm_all = bf16[8,32,2048]{2,1,0:T(8,128)(2,1)S(1)} async-done(((bf16[8,32,2048]{2,1,0:T(8,128)(2,1)}), bf16[8,32,2048]{2,1,0:T(8,128)(2,1)S(1)}, u32[]{:S(2)}, u32[]{:S(2)}) %all-to-all-start.9) | async-done | bytes 1048608 | tf_op jit(solution)/shard_map/all_to_all | solution.py:53
  158.4 24.2 %all_to_all.68.parts = bf16[4,512,384]{2,1,0:T(8,128)(2,1)} all-to-all(bf16[4,512,384]{2,1,0:T(8,128)(2,1)} %copy-done.7), channel_id=1, replica_groups=mesh['y'=4,'xl'=2,'z'=8,'c'=2,'e'=2] {'y'}, dimensions={0} | all-to-all | bytes 3145728 | tf_op jit(solution)/shard_map/all_to_all | solution.py:53
  182.6 6.1 %all-to-all-start.7 = ((bf16[8,32,2048]{2,1,0:T(8,128)(2,1)}), bf16[8,32,2048]{2,1,0:T(8,128)(2,1)}, u32[]{:S(2)}, u32[]{:S(2)}) async-start(bf16[8,32,2048]{2,1,0:T(8,128)(2,1)} %copy-done.11), calls=%async_computation.7 | async-start | bytes 2097152 | tf_op jit(solution)/shard_map/all_to_all | solution.py:53
  191.0 12.8 %all-to-all-done.7.z_parts = bf16[8,32,2048]{2,1,0:T(8,128)(2,1)} async-done(((bf16[8,32,2048]{2,1,0:T(8,128)(2,1)}), bf16[8,32,2048]{2,1,0:T(8,128)(2,1)}, u32[]{:S(2)}, u32[]{:S(2)}) %all-to-all-start.7) | async-done | bytes 1048608 | tf_op jit(solution)/shard_map/all_to_all | solution.py:53
  203.7 4.1 %all-to-all-start.11 = ((bf16[8,2,32,384]{3,2,1,0:T(8,128)(2,1)}), bf16[8,2,32,384]{3,2,1,0:T(8,128)(2,1)}, u32[]{:S(2)}, u32[]{:S(2)}) async-start(bf16[8,2,32,384]{3,2,1,0:T(8,128)(2,1)} %copy-done.8), calls=%async_computation.11 | async-start | bytes 786432 | tf_op jit(solution)/shard_map/all_to_all | solution.py:53
  212.8 10.2 %all-to-all-done.11.parts = bf16[8,2,32,384]{3,2,1,0:T(8,128)(2,1)} async-done(((bf16[8,2,32,384]{3,2,1,0:T(8,128)(2,1)}), bf16[8,2,32,384]{3,2,1,0:T(8,128)(2,1)}, u32[]{:S(2)}, u32[]{:S(2)}) %all-to-all-start.11) | async-done | bytes 393248 | tf_op jit(solution)/shard_map/all_to_all | solution.py:53
  223.0 4.2 %all-to-all-start.8 = ((bf16[8,32,2048]{2,1,0:T(8,128)(2,1)}), bf16[8,32,2048]{2,1,0:T(8,128)(2,1)}, u32[]{:S(2)}, u32[]{:S(2)}) async-start(bf16[8,32,2048]{2,1,0:T(8,128)(2,1)} %copy-done), calls=%async_computation.8 | async-start | bytes 2097152 | tf_op jit(solution)/shard_map/all_to_all | solution.py:53
  228.9 13.7 %all-to-all-done.8.da_all = bf16[8,32,2048]{2,1,0:T(8,128)(2,1)} async-done(((bf16[8,32,2048]{2,1,0:T(8,128)(2,1)}), bf16[8,32,2048]{2,1,0:T(8,128)(2,1)}, u32[]{:S(2)}, u32[]{:S(2)}) %all-to-all-start.8) | async-done | bytes 1048608 | tf_op jit(solution)/shard_map/all_to_all | solution.py:53
  242.6 4.6 %all-to-all-start.12 = ((f32[4,16,384]{2,1,0:T(8,128)}), f32[4,16,384]{2,1,0:T(8,128)S(1)}, u32[]{:S(2)}, u32[]{:S(2)}) async-start(f32[4,16,384]{2,1,0:T(8,128)} %bitcast.18), calls=%async_computation.12 | async-start | bytes 196608 | tf_op jit(solution)/shard_map/all_to_all | solution.py:53
  249.6 5.7 %shard_map.153 = bf16[128,2048]{1,0:T(8,128)(2,1)} custom-call(bf16[8,32,2048]{2,1,0:T(8,128)(2,1)S(1)} %copy-done.1, bf16[128,2048]{1,0:T(8,128)(2,1)S(1)} %bitcast.26, bf16[128,2048]{1,0:T(8,128)(2,1)S(1)} %bitcast.29, s32[1,32]{1,0:T(1,128)S(1)} %bitcast.38, f32[32,16]{1,0:T(8,128)S(1)} %get-tuple-element.30.cm, f32[16,128]{1,0:T(8,128)S(1)} %get-tuple-element.25.cum, ...), custom_call_target="tpu_custom_call" | custom-call | flops 100000000 | bytes 3688576 | tf_op jit(solution)/shard_map/pallas_call | solution.py:22
  255.3 4.8 %shard_map.155 = (bf16[128,2048]{1,0:T(8,128)(2,1)}, bf16[128,2048]{1,0:T(8,128)(2,1)}) custom-call(bf16[8,32,2048]{2,1,0:T(8,128)(2,1)} %all-to-all-done.8.da_all, bf16[8,32,2048]{2,1,0:T(8,128)(2,1)S(1)} %all-to-all-done.9.qm_all, bf16[128,2048]{1,0:T(8,128)(2,1)S(1)} %bitcast.30, f32[16,128,256]{2,1,0:T(8,128)S(1)} %get-tuple-element.38.decay, ...), custom_call_target="tpu_custom_call" | custom-call | flops 100000000 | bytes 6815744 | tf_op jit(solution)/shard_map/pallas_call | solution.py:22
  (76 shorter events, 36.4 us)
Async XLA Ops:
  0.6 17.9 %copy-start.25 = (s32[1,1,32]{2,1,0:T(1,128)S(1)}, s32[1,1,32]{2,1,0:T(1,128)}, u32[]{:S(2)}) copy-start(s32[1,1,32]{2,1,0:T(1,128)} %param.17) | copy-start | bytes 388
  0.6 18.0 %copy-start.2 = (bf16[1,128,2048]{2,1,0:T(8,128)(2,1)S(1)}, bf16[1,128,2048]{2,1,0:T(8,128)(2,1)}, u32[]{:S(2)}) copy-start(bf16[1,128,2048]{2,1,0:T(8,128)(2,1)} %param.13) | copy-start | bytes 1572868
  0.7 18.0 %copy-start.4 = (bf16[1,128,2048]{2,1,0:T(8,128)(2,1)S(1)}, bf16[1,128,2048]{2,1,0:T(8,128)(2,1)}, u32[]{:S(2)}) copy-start(bf16[1,128,2048]{2,1,0:T(8,128)(2,1)} %param.14) | copy-start | bytes 1572868
  0.7 18.0 %copy-start.24 = (f32[1,16,128]{2,1,0:T(8,128)S(1)}, f32[1,16,128]{2,1,0:T(8,128)}, u32[]{:S(2)}) copy-start(f32[1,16,128]{2,1,0:T(8,128)} %param.15) | copy-start | bytes 24580
  11.9 20.3 %all-to-all-start.5 = ((bf16[8,64,384]{2,1,0:T(8,128)(2,1)}), bf16[8,64,384]{2,1,0:T(8,128)(2,1)}, u32[]{:S(2)}, u32[]{:S(2)}) async-start(bf16[8,64,384]{2,1,0:T(8,128)(2,1)} %broadcast_in_dim.40), calls=%async_computation.5 | async-start | bytes 786432 | tf_op jit(solution)/shard_map/all_to_all | solution.py:53
  18.7 17.7 %copy-start.13 = (bf16[1,128,2048]{2,1,0:T(8,128)(2,1)S(1)}, bf16[1,128,2048]{2,1,0:T(8,128)(2,1)}, u32[]{:S(2)}) copy-start(bf16[1,128,2048]{2,1,0:T(8,128)(2,1)} %param.12) | copy-start | bytes 1572868
  18.7 17.7 %copy-start.14 = (bf16[1,128,2048]{2,1,0:T(8,128)(2,1)S(1)}, bf16[1,128,2048]{2,1,0:T(8,128)(2,1)}, u32[]{:S(2)}) copy-start(bf16[1,128,2048]{2,1,0:T(8,128)(2,1)} %param.11) | copy-start | bytes 1572868
  18.7 17.7 %copy-start.15 = (bf16[1,1,32,2048]{3,2,1,0:T(8,128)(2,1)S(1)}, bf16[1,1,32,2048]{3,2,1,0:T(8,128)(2,1)}, u32[]{:S(2)}) copy-start(bf16[1,1,32,2048]{3,2,1,0:T(8,128)(2,1)} %param.16) | copy-start | bytes 393220
  18.7 17.7 %copy-start.26 = (s32[1,1,2,128]{3,2,1,0:T(2,128)S(1)}, s32[1,1,2,128]{3,2,1,0:T(2,128)}, u32[]{:S(2)}) copy-start(s32[1,1,2,128]{3,2,1,0:T(2,128)} %param.18) | copy-start | bytes 3076
  18.7 17.7 %copy-start.27 = (f32[1,1,2,128]{3,2,1,0:T(2,128)S(1)}, f32[1,1,2,128]{3,2,1,0:T(2,128)}, u32[]{:S(2)}) copy-start(f32[1,1,2,128]{3,2,1,0:T(2,128)} %param.19) | copy-start | bytes 3076
  32.2 18.0 %all-to-all-start = ((bf16[8,528,128]{2,1,0:T(8,128)(2,1)}), bf16[8,528,128]{2,1,0:T(8,128)(2,1)S(1)}, u32[]{:S(2)}, u32[]{:S(2)}) async-start(bf16[8,528,128]{2,1,0:T(8,128)(2,1)} %get-tuple-element.31), calls=%async_computation | async-start | bytes 2162688 | tf_op jit(solution)/shard_map/all_to_all | solution.py:53
  50.2 22.3 %all-to-all-start.3 = ((bf16[8,32,2048]{2,1,0:T(8,128)(2,1)}), bf16[8,32,2048]{2,1,0:T(8,128)(2,1)S(1)}, u32[]{:S(2)}, u32[]{:S(2)}) async-start(bf16[8,32,2048]{2,1,0:T(8,128)(2,1)} %get-tuple-element.33), calls=%async_computation.3 | async-start | bytes 2097152 | tf_op jit(solution)/shard_map/all_to_all | solution.py:53
  93.7 24.0 %all-to-all-start.6 = ((bf16[4,512,384]{2,1,0:T(8,128)(2,1)}), bf16[4,512,384]{2,1,0:T(8,128)(2,1)}, u32[]{:S(2)}, u32[]{:S(2)}) async-start(bf16[4,512,384]{2,1,0:T(8,128)(2,1)} %broadcast_in_dim.42), calls=%async_computation.6 | async-start | bytes 3145728 | tf_op jit(solution)/shard_map/all_to_all | solution.py:53
  139.0 19.4 %all-to-all-start.9 = ((bf16[8,32,2048]{2,1,0:T(8,128)(2,1)}), bf16[8,32,2048]{2,1,0:T(8,128)(2,1)S(1)}, u32[]{:S(2)}, u32[]{:S(2)}) async-start(bf16[8,32,2048]{2,1,0:T(8,128)(2,1)} %broadcast_in_dim.44), calls=%async_computation.9 | async-start | bytes 2097152 | tf_op jit(solution)/shard_map/all_to_all | solution.py:53
  142.6 1.2 copy-start.10
  143.8 1.2 copy-start.12
  149.5 1.1 copy-start.7
  182.6 21.2 %all-to-all-start.7 = ((bf16[8,32,2048]{2,1,0:T(8,128)(2,1)}), bf16[8,32,2048]{2,1,0:T(8,128)(2,1)}, u32[]{:S(2)}, u32[]{:S(2)}) async-start(bf16[8,32,2048]{2,1,0:T(8,128)(2,1)} %copy-done.11), calls=%async_computation.7 | async-start | bytes 2097152 | tf_op jit(solution)/shard_map/all_to_all | solution.py:53
  188.6 1.4 copy-start.6
  203.7 19.3 %all-to-all-start.11 = ((bf16[8,2,32,384]{3,2,1,0:T(8,128)(2,1)}), bf16[8,2,32,384]{3,2,1,0:T(8,128)(2,1)}, u32[]{:S(2)}, u32[]{:S(2)}) async-start(bf16[8,2,32,384]{3,2,1,0:T(8,128)(2,1)} %copy-done.8), calls=%async_computation.11 | async-start | bytes 786432 | tf_op jit(solution)/shard_map/all_to_all | solution.py:53
  223.0 19.6 %all-to-all-start.8 = ((bf16[8,32,2048]{2,1,0:T(8,128)(2,1)}), bf16[8,32,2048]{2,1,0:T(8,128)(2,1)}, u32[]{:S(2)}, u32[]{:S(2)}) async-start(bf16[8,32,2048]{2,1,0:T(8,128)(2,1)} %copy-done), calls=%async_computation.8 | async-start | bytes 2097152 | tf_op jit(solution)/shard_map/all_to_all | solution.py:53
  242.6 17.5 %all-to-all-start.12 = ((f32[4,16,384]{2,1,0:T(8,128)}), f32[4,16,384]{2,1,0:T(8,128)S(1)}, u32[]{:S(2)}, u32[]{:S(2)}) async-start(f32[4,16,384]{2,1,0:T(8,128)} %bitcast.18), calls=%async_computation.12 | async-start | bytes 196608 | tf_op jit(solution)/shard_map/all_to_all | solution.py:53
  248.3 1.2 copy-start.1
  248.3 1.4 copy-start.5
  (15 other events, 12.9 us)

commit v2 on v1

--- a/solution.py
+++ b/solution.py
@@ -10,12 +10,13 @@
 EPS = 1e-05
 SEQ = ("y", "xl")
 GRP = ("xl", "c", "e")
+Y, XL, Z, C, E = range(5)
 F32 = jnp.float32
 BF16 = jnp.bfloat16
 HIGH = lax.Precision.HIGHEST
 
 
-def call(body, outs, *args, flops=10**8, scalar=False):
+def call(body, outs, *args, flops=10**8, scalar=False, scratch=()):
     shapes = [jax.ShapeDtypeStruct(s, d) for s, d in outs]
     moved = sum(a.size * a.dtype.itemsize for a in (*args, *shapes))
     spaces = [pltpu.SMEM if scalar and k == 0 else pltpu.VMEM for k in range(len(args))]
@@ -23,7 +24,8 @@
         body,
         out_shape=shapes,
         in_specs=[pl.BlockSpec(memory_space=m) for m in spaces],
-        compiler_params=pltpu.CompilerParams(vmem_limit_bytes=44 << 20),
+        scratch_shapes=list(scratch),
+        compiler_params=pltpu.CompilerParams(vmem_limit_bytes=20 << 20),
         cost_estimate=pl.CostEstimate(flops=flops, bytes_accessed=moved, transcendentals=0),
     )(*args)
     return result
@@ -53,11 +55,7 @@
     return lax.all_to_all(x, axes, split_axis=0, concat_axis=0, tiled=True)
 
 
-def broadcast(x, axes, n):
-    return exchange(jnp.broadcast_to(x[None], (n, *x.shape)), axes)
-
-
-def weights_body(up, down, out):
+def prepare_body(ids, up, down, cot, mask, routes, gates, w0, w1, w2, w3, own_out, other_out, slices):
     low = iota((up.shape[0], HD), 1) < 64
     for c in range(12):
         u = up[:, head(c // 2)].astype(F32)
@@ -66,7 +64,22 @@
             u = pltpu.roll(u, 64, 1)
         else:
             d = pltpu.roll(d, 64, 1)
-        out[c // 3, :, head(c % 3)] = jnp.where(low, u, d).astype(BF16)
+        slices[c // 3, :, head(c % 3)] = jnp.where(low, u, d).astype(BF16)
+    for k, w in enumerate((w0, w1, w2, w3)):
+        w[...] = slices[(ids[XL] * 2 + ids[C]) ^ k]
+    lane = iota((HD, HD), 1)
+    sub = iota((HD, HD), 0)
+    table = jnp.zeros((HD, HD), F32)
+    for e in range(2):
+        hit = jnp.where(sub == routes[e : e + 1, :], gates[e : e + 1, :], 0.0)
+        table = jnp.where(lane == e, jnp.sum(hit, axis=1, keepdims=True), table)
+    pick_f = (iota((HD, 32), 0) == mask[...]).astype(F32)
+    gm = tn(pick_f, table, precision=HIGH)
+    cotf = cot[...].astype(F32)
+    first, second = (gm[:, 0:1] * cotf).astype(BF16), (gm[:, 1:2] * cotf).astype(BF16)
+    swap = ids[E] == 1
+    own_out[...] = jnp.where(swap, second, first)
+    other_out[...] = jnp.where(swap, first, second)
 
 
 def weight_grads_body(scale, g, up, down):
@@ -109,43 +122,28 @@
         out[g, 512:528, :] = packed
 
 
-def masked_body(
-    query, key, value, residual, cot, mask, routes, gates, cum, cum_t, qm_out, rm_out, inner_out, sg_out, cm_out
-):
+def masked_body(query, key, value, residual, mask, cum, cum_t, qm_out, rm_out, inner_out, cm_out):
     pick_t = (iota((HD, 32), 0) == mask[...]).astype(BF16)
     qm = tn(pick_t, query[...]).astype(BF16)
     qm_out[...] = qm
     rm_out[...] = tn(pick_t, residual[...])
-    lane = iota((HD, HD), 1)
-    sub = iota((HD, HD), 0)
-    pick_f = pick_t.astype(F32)
-    cm = tn(pick_f, cum_t[...], precision=HIGH)
+    cm = tn(pick_t.astype(F32), cum_t[...], precision=HIGH)
     cm_out[...] = cm
     cumv = cum[...]
     for h in range(HEADS):
         s = nt(qm[:, head(h)], key[:, head(h)])
         p = (s * jnp.exp(-jnp.abs(cm[:, h : h + 1] - cumv[h : h + 1, :]))).astype(BF16)
         inner_out[:, head(h)] = nn(p, value[:, head(h)])
-    table = jnp.zeros((HD, HD), F32)
-    for e in range(2):
-        hit = jnp.where(sub == routes[e : e + 1, :], gates[e : e + 1, :], 0.0)
-        table = jnp.where(lane == e, jnp.sum(hit, axis=1, keepdims=True), table)
-    gm = tn(pick_f, table, precision=HIGH)
-    cotf = cot[...].astype(F32)
-    for e in range(2):
-        sg = (gm[:, e : e + 1] * cotf).astype(BF16)
-        for k in range(4):
-            sg_out[2 * k + e] = sg
-
-
-def carry_body(mine, parts, out):
+
+
+def carry_body(ids, parts, out):
     row, lane = iota((HEADS, HD), 0), iota((HEADS, HD), 1)
     ends = (lane >= 96) & (lane < 99)
     n = parts.shape[0]
     for j in range(2):
         at = slice(j * HD, (j + 1) * HD)
         back = slice(256 + j * HD, 256 + (j + 1) * HD)
-        wanted = ends & (row == 2 * mine[0] + j)
+        wanted = ends & (row == 2 * (2 * ids[Y] + ids[XL]) + j)
         decay = [
             jnp.exp(jnp.sum(jnp.where(wanted, parts[a, 512:528, :].astype(F32), 0.0), keepdims=True))
             for a in range(n)
@@ -194,14 +192,21 @@
             routed_out[k, :, head(h)] = routed
 
 
-def expert_body(rows, grads, weights, z_out, dw_out, w_ref):
-    ny, nz, nx, unit = weights.shape[:4]
-    for y in range(ny):
-        for z in range(nz):
-            for x in range(nx):
-                w_ref[pl.ds(((y * nx + x) * nz + z) * unit, unit), :] = weights[y, z, x]
-    r = rows[...].reshape(256, HEADS * HD)
-    g = grads[...].reshape(256, HEADS * HD)
+def expert_body(ids, rows, grads, w0, w1, w2, w3, z_out, d0, d1, d2, d3, w_ref, g_ref):
+    nz, unit = w0.shape[0], w0.shape[2]
+    for k, piece in enumerate((w0, w1, w2, w3)):
+        y = (ids[Y] + 4 - k) % 4
+        for zs in range(nz):
+            for cs in range(4):
+                x = ids[XL] ^ (cs // 2)
+                at = (((y * 2 + x) * nz + (ids[Z] ^ zs)) * 2 + (ids[C] ^ (cs % 2))) * unit
+                w_ref[pl.ds(pl.multiple_of(at, unit), unit), :] = piece[zs, cs]
+    for k in range(8):
+        slot = ((k % 2) ^ ids[E]) + 2 * ((k // 4) ^ ids[XL]) + 4 * ((k // 2 % 2) ^ ids[C])
+        g_ref[k] = grads[slot]
+    width = HEADS * HD
+    r = rows[...].reshape(256, width)
+    g = g_ref[...].reshape(256, width)
     w = w_ref[...]
     pre_all = nn(r, w)
     grad_all = nn(g, w)
@@ -219,21 +224,19 @@
     ac = jnp.concatenate(acts, axis=1)
     z_out[...] = nt(pg, w).astype(BF16).reshape(z_out.shape)
     both = jnp.concatenate((pg, ac), axis=0)
-    for y in range(4):
-        cols = slice(y * 512, (y + 1) * 512)
-        sides = jnp.concatenate((r[:, cols], g[:, cols]), axis=0)
-        dw_out[y] = tn(sides, both).astype(BF16)
-
-
-def sum_y_body(parts, out):
-    ny = parts.shape[0]
+    for k, out in enumerate((d0, d1, d2, d3)):
+        y = (ids[Y] + k) % 4
+        cols = pl.ds(pl.multiple_of(y * 512, 512), 512)
+        sides = jnp.concatenate((rows[:, :, cols].reshape(256, 512), g_ref[:, :, cols].reshape(256, 512)), axis=0)
+        out[...] = tn(sides, both).astype(BF16)
+
+
+def sum_y_body(p0, p1, p2, p3, out):
     nz, nx, unit = out.shape[:3]
     for x in range(nx):
         for z in range(nz):
             at = slice((x * nz + z) * unit, (x * nz + z + 1) * unit)
-            total = parts[0, at, :].astype(F32)
-            for y in range(1, ny):
-                total = total + parts[y, at, :].astype(F32)
+            total = p0[at, :].astype(F32) + p1[at, :].astype(F32) + p2[at, :].astype(F32) + p3[at, :].astype(F32)
             out[z, x] = total.astype(BF16)
 
 
@@ -256,13 +259,11 @@
         n = normed[:, head(h)]
         g = rg[:, head(h)]
         m = jnp.mean(g * n, axis=-1, keepdims=True)
-        a = (st[:, h : h + 1] * (g - n * m)).astype(BF16)
-        for k in range(8):
-            out[k, :, head(h)] = a
-
-
-def query_grad_body(da8, key, value, mask, cm, cum, cum_t, carried, out):
-    da = da8[0]
+        out[:, head(h)] = (st[:, h : h + 1] * (g - n * m)).astype(BF16)
+
+
+def query_grad_body(da_own, key, value, mask, cm, cum, cum_t, carried, out):
+    da = da_own[...]
     pick_t = (iota((HD, 32), 0) == mask[...]).astype(BF16)
     cmv = cm[...]
     cumv = cum[...]
@@ -277,11 +278,18 @@
         out[:, head(h)] = nn(pick_t, q.astype(BF16)).astype(BF16)
 
 
-def scores_body(mine, parts, qm_all, key, cum_t, decay_out, scores_out):
+def rows_of(pieces, h):
+    return jnp.concatenate([p[:, :, head(h)].reshape(64, HD) for p in pieces], axis=0)
+
+
+def scores_body(ids, parts, q0, q1, q2, q3, key, cum_t, decay_out, scores_out):
     n = parts.shape[0]
     lane, col = iota((HD, n * 32), 0), iota((HD, n * 32), 1)
-    block = col // 32
-    me = mine[0]
+    me = 2 * ids[Y] + ids[XL]
+    block = jnp.zeros((HD, n * 32), jnp.int32)
+    for k in range(n):
+        there = 2 * ((ids[Y] + 4 - k // 2) % 4) + (ids[XL] ^ (k % 2))
+        block = jnp.where(col // 32 == k, there, block)
     at = jnp.zeros((HEADS, n * 32), F32)
     for a in range(n):
         own = (lane < 96) & (lane % 32 == col % 32) & (block == a)
@@ -294,18 +302,33 @@
     for h in range(HEADS):
         decay = jnp.exp(-jnp.abs(ct[:, h : h + 1] - at[h : h + 1, :]))
         decay_out[h] = decay
-        qm = qm_all[:, :, head(h)].reshape(n * 32, HD)
-        scores_out[h] = (nt(key[:, head(h)], qm) * decay).astype(BF16)
-
-
-def key_value_grads_body(da_all, qm_all, value, decay, scores, key_out, value_out):
-    rows = da_all.shape[0] * 32
-    for h in range(HEADS):
-        da = da_all[:, :, head(h)].reshape(rows, HD)
-        qm = qm_all[:, :, head(h)].reshape(rows, HD)
+        scores_out[h] = (nt(key[:, head(h)], rows_of((q0, q1, q2, q3), h)) * decay).astype(BF16)
+
+
+def key_value_grads_body(a0, a1, a2, a3, q0, q1, q2, q3, value, decay, scores, key_out, value_out):
+    for h in range(HEADS):
+        da = rows_of((a0, a1, a2, a3), h)
         value_out[:, head(h)] = nn(scores[h], da).astype(BF16)
         p = (nt(value[:, head(h)], da) * decay[h]).astype(BF16)
-        key_out[:, head(h)] = nn(p, qm).astype(BF16)
+        key_out[:, head(h)] = nn(p, rows_of((q0, q1, q2, q3), h)).astype(BF16)
+
+
+def trade(x, axis, bit=1):
+    n = lax.axis_size(axis)
+    return lax.ppermute(x, axis, [(i, i ^ bit) for i in range(n)])
+
+
+def turn(x, k):
+    n = lax.axis_size("y")
+    return lax.ppermute(x, "y", [(i, (i + k) % n) for i in range(n)])
+
+
+def along_y(x):
+    return [x] + [turn(x, k) for k in range(1, 4)]
+
+
+def along_sequence(x):
+    return along_y(jnp.stack((x, trade(x, "xl"))))
 
 
 def local(residual, query, key, value, ld, cot, mask, routes, gates, up, down):
@@ -314,56 +337,76 @@
     width = HEADS * HD
     ny, nx, nz, nc = (lax.axis_size(a) for a in ("y", "xl", "z", "c"))
     shard = up.shape[0]
-    mine = (lax.axis_index("y") * nx + lax.axis_index("xl")).astype(jnp.int32).reshape(1)
+    ids = jnp.stack([lax.axis_index(a) for a in ("y", "xl", "z", "c", "e")]).astype(jnp.int32)
     places = jnp.concatenate((mask, mask, mask, jnp.full_like(mask, HD - 1)), axis=1)
 
-    [w0] = call(weights_body, [((4, shard, 384), BF16)], up, down)
+    prepared = call(
+        prepare_body,
+        [((shard, 384), BF16)] * 4 + [((32, width), BF16)] * 2,
+        ids, up, down, cot, mask, routes, gates,
+        scalar=True,
+        scratch=[pltpu.VMEM((4, shard, 384), BF16)],
+    )
+    w = [prepared[0]] + [
+        lax.ppermute(prepared[k], ("xl", "c"), [(i, i ^ k) for i in range(4)]) for k in range(1, 4)
+    ]
+    grads = jnp.stack((prepared[4], trade(prepared[5], "e")))
     states, cum, cum_t = call(
         states_body,
         [((8, 528, HD), BF16), ((HEADS, HD), F32), ((HD, HEADS), F32)],
         ld, key, value, places,
     )
     parts = exchange(states, SEQ)
-    w1 = exchange(w0, ("xl", "c"))
-    qm, rm, inner, sg, cm = call(
+    qm, rm, inner, cm = call(
         masked_body,
-        [((32, width), BF16), ((32, width), F32), ((32, width), F32), ((8, 32, width), BF16), ((32, HEADS), F32)],
-        query, key, value, residual, cot, mask, routes, gates, cum, cum_t,
-    )
-    [carries] = call(carry_body, [((8, 512, HD), BF16)], mine, parts, scalar=True)
+        [((32, width), BF16), ((32, width), F32), ((32, width), F32), ((32, HEADS), F32)],
+        query, key, value, residual, mask, cum, cum_t,
+    )
+    [carries] = call(carry_body, [((8, 512, HD), BF16)], ids, parts, scalar=True)
     carried = exchange(carries, SEQ)
-    w2 = broadcast(w1.reshape(4 * shard, 384), "z", nz)
-    w3 = broadcast(w2.reshape(nz * 4 * shard, 384), "y", ny)
-    grads = exchange(sg, GRP)
+    grads = jnp.concatenate((grads, trade(grads, "xl")))
+    grads = jnp.concatenate((grads, trade(grads, "c")))
+    w = jnp.stack(w)[None]
+    bit = 1
+    while bit < nz:
+        w = jnp.concatenate((w, trade(w, "z", bit)))
+        bit *= 2
     routed8, normed, normalized, stats = call(
         rows_body,
         [((8, 32, width), BF16), ((32, width), F32), ((32, width), F32), ((32, HD), F32)],
         qm, rm, inner, cm, cum_t, carried,
     )
+    weights = along_y(w)
     rows = exchange(routed8, GRP)
-    weights = w3.reshape(ny, nz, nx, nc * shard, 384)
-    z_send, dw = expert_call(rows, grads, weights, ny)
+    z_send, *dw = call(
+        expert_body,
+        [((8, 32, width), BF16)] + [((width // ny, 384), BF16)] * 4,
+        ids, rows, grads, *weights,
+        scalar=True,
+        scratch=[pltpu.VMEM((width, 384), BF16), pltpu.VMEM((8, 32, width), BF16)],
+        flops=2 * 10**9,
+    )
     z_parts = exchange(z_send, GRP)
-    [da8] = call(grads_body, [((8, 32, width), BF16)], z_parts, cot, normed, normalized, stats)
-    da_all = exchange(da8, SEQ)
-    qm_all = broadcast(qm, SEQ, 8)
-    [query_grad] = call(query_grad_body, [((HD, width), BF16)], da8, key, value, mask, cm, cum, cum_t, carried)
+    queries = along_sequence(qm)
+    d1 = [dw[0]] + [turn(dw[k], k) for k in range(1, 4)]
     decay, scores = call(
         scores_body,
         [((HEADS, HD, 256), F32), ((HEADS, HD, 256), BF16)],
-        mine, parts, qm_all, key, cum_t,
+        ids, parts, *queries, key, cum_t,
         scalar=True,
     )
+    [da] = call(grads_body, [((32, width), BF16)], z_parts, cot, normed, normalized, stats)
+    das = along_sequence(da)
+    [d2] = call(sum_y_body, [((nz, nx, nc * shard, 384), BF16)], *d1)
+    d3 = exchange(d2, "z")
+    [query_grad] = call(query_grad_body, [((HD, width), BF16)], da, key, value, mask, cm, cum, cum_t, carried)
+    [d4] = call(sum_z_body, [((nx, nc * shard, 384), F32)], d3)
+    d5 = exchange(d4.reshape(4, shard, 384), ("xl", "c"))
     key_grad, value_grad = call(
         key_value_grads_body,
         [((HD, width), BF16), ((HD, width), BF16)],
-        da_all, qm_all, value, decay, scores,
-    )
-    d1 = exchange(dw, "y")
-    [d2] = call(sum_y_body, [((nz, nx, nc * shard, 384), BF16)], d1)
-    d3 = exchange(d2, "z")
-    [d4] = call(sum_z_body, [((nx, nc * shard, 384), F32)], d3)
-    d5 = exchange(d4.reshape(4, shard, 384), ("xl", "c"))
+        *das, *queries, value, decay, scores,
+    )
     scale = 1.0 / (ny * nx * nz * nc)
 
     def finish(g, a, b):
@@ -371,22 +414,6 @@
 
     up_grad, down_grad = call(finish, [((shard, 768), F32), ((shard, 768), F32)], d5)
     return query_grad[None], key_grad[None], value_grad[None], up_grad[None], down_grad[None]
-
-
-def expert_call(rows, grads, weights, ny):
-    width = rows.shape[2]
-    outs = [
-        jax.ShapeDtypeStruct(rows.shape, BF16),
-        jax.ShapeDtypeStruct((ny, width // ny, 384), BF16),
-    ]
-    moved = sum(a.size * a.dtype.itemsize for a in (rows, grads, weights, *outs))
-    return pl.pallas_call(
-        expert_body,
-        out_shape=outs,
-        scratch_shapes=[pltpu.VMEM((width, 384), BF16)],
-        compiler_params=pltpu.CompilerParams(vmem_limit_bytes=44 << 20),
-        cost_estimate=pl.CostEstimate(flops=2 * 10**9, bytes_accessed=moved, transcendentals=0),
-    )(rows, grads, weights)
 
 
 def solution(mesh):

time: 262 us -> 212 us (0.81)
  blocking collectives: 71.1 us -> 0 us
  waiting for transfers between devices: 91.9 us -> 60.2 us
  starting transfers between devices: 45.1 us -> 73.8 us
  local copies, waits for them, and re-layouts: 22.6 us -> 36.7 us
  other arithmetic: 0.08 us -> 8.95 us
    all_to_all x9 -> x6, waiting for transfers between devices: 91.9 us -> 14.8 us  [exchange(): return lax.all_to_all(x, axes, split_axis=0, concat_axis=0, tiled=True)]
    all_to_all x4 -> x0, blocking collectives: 71.1 us -> none  [exchange(): return lax.all_to_all(x, axes, split_axis=0, concat_axis=0, tiled=True)]
    ppermute x0 -> x23, waiting for transfers between devices: none -> 45.4 us  [the longest x12 30 us: turn(): return lax.ppermute(x, 'y', [(i, (i + k) % n) for i in range(n)])]
    ppermute x0 -> x23, starting transfers between devices: none -> 35 us  [the longest x12 16.6 us: turn(): return lax.ppermute(x, 'y', [(i, (i + k) % n) for i in range(n)])]
    unnamed x60 -> x118, local copies, waits for them, and re-layouts: 18.5 us -> 36.6 us
    all_to_all x9 -> x6, starting transfers between devices: 45.1 us -> 38.7 us  [exchange(): return lax.all_to_all(x, axes, split_axis=0, concat_axis=0, tiled=True)]
    concatenate x0 -> x5, other arithmetic: none -> 5.67 us  [the longest x3 2.56 us: local(): w = jnp.concatenate((w, trade(w, 'z', bit)))]
    pallas_call x12 -> x13, Pallas kernels: 24.8 us -> 29.6 us  [call(): pl.pallas_call(body, out_shape=shapes, in_specs=[pl.BlockSpec(memory_spac...]
  transfers between devices with their start and end apart: 9 -> 29, of which waited for: 8 -> 9; matrix products, arithmetic and copies ran while one was open for 0% -> 4% of each run, Pallas kernels for 11% -> 8%
where the time goes in v2:
time: 212 us; the launch traced here: 210 us
  starting transfers between devices  73.8 us (35%)
  waiting for transfers between devices  60.2 us (28%)
  local copies, waits for them, and re-layouts  36.7 us (17%)
  Pallas kernels  29.6 us (14%)
  other arithmetic  8.95 us (4%)
    all_to_all x6, starting transfers between devices, exchange(): return lax.all_to_all(x, axes, split_axis=0, concat_axis=0, tiled=True)  38.7 us
    unnamed x118, local copies, waits for them, and re-layouts  36.6 us
    ppermute x12, waiting for transfers between devices, turn(): return lax.ppermute(x, 'y', [(i, (i + k) % n) for i in range(n)])  30 us
    pallas_call x13, Pallas kernels, call(): pl.pallas_call(body, out_shape=shapes, in_specs=[pl.BlockSpec(memory_spac...  29.6 us
    ppermute x12, starting transfers between devices, turn(): return lax.ppermute(x, 'y', [(i, (i + k) % n) for i in range(n)])  16.6 us
    ppermute x8, waiting for transfers between devices, trade(): return lax.ppermute(x, axis, [(i, i ^ bit) for i in range(n)])  15.4 us
    ppermute x8, starting transfers between devices, trade(): return lax.ppermute(x, axis, [(i, i ^ bit) for i in range(n)])  14.9 us
    all_to_all x6, waiting for transfers between devices, exchange(): return lax.all_to_all(x, axes, split_axis=0, concat_axis=0, tiled=True)  14.8 us
  transfers between devices with their start and end apart: 29, of which 9 were waited for; matrix products, arithmetic and copies ran while one was open for 4% of the time, Pallas kernels for 8%

profile of v2, /device:TPU:1, one launch (start us, length us, event | category | flops | bytes accessed | tf_op | source)
XLA Modules:
  0.0 210.1 jit_solution(6397763293206712866)
XLA Ops:
  7.1 5.9 %all-to-all-start = ((bf16[8,528,128]{2,1,0:T(8,128)(2,1)}), bf16[8,528,128]{2,1,0:T(8,128)(2,1)S(1)}, u32[]{:S(2)}, u32[]{:S(2)}) async-start(bf16[8,528,128]{2,1,0:T(8,128)(2,1)} %copy-done.10), calls=%async_computation | async-start | bytes 2162688 | tf_op jit(solution)/shard_map/all_to_all | solution.py:55
  13.1 14.8 %all-to-all-done.parts = bf16[8,528,128]{2,1,0:T(8,128)(2,1)S(1)} async-done(((bf16[8,528,128]{2,1,0:T(8,128)(2,1)}), bf16[8,528,128]{2,1,0:T(8,128)(2,1)S(1)}, u32[]{:S(2)}, u32[]{:S(2)}) %all-to-all-start) | async-done | bytes 1081376 | tf_op jit(solution)/shard_map/all_to_all | solution.py:55
  29.8 4.3 %all-to-all-start.1 = ((bf16[8,512,128]{2,1,0:T(8,128)(2,1)}), bf16[8,512,128]{2,1,0:T(8,128)(2,1)S(1)}, u32[]{:S(2)}, u32[]{:S(2)}) async-start(bf16[8,512,128]{2,1,0:T(8,128)(2,1)} %copy-done.4), calls=%async_computation.1 | async-start | bytes 2097152 | tf_op jit(solution)/shard_map/all_to_all | solution.py:55
  36.6 2.5 %collective-permute-start = (bf16[32,2048]{1,0:T(8,128)(2,1)S(1)}, bf16[32,2048]{1,0:T(8,128)(2,1)S(1)}, u32[]{:S(2)}, u32[]{:S(2)}) collective-permute-start(bf16[32,2048]{1,0:T(8,128)(2,1)S(1)} %get-tuple-element.42), channel_id=1, source_target_pairs={{0,1},{1,0},{2,3},{3,2},{4,5},{5,4},{6,7},{7,6},{8,9},{9,8},{10,11... | collective-permute-start | bytes 393224 | tf_op jit(solution)/shard_map/ppermute | solution.py:318
  42.6 7.6 %collective-permute-done = bf16[32,2048]{1,0:T(8,128)(2,1)S(1)} collective-permute-done((bf16[32,2048]{1,0:T(8,128)(2,1)S(1)}, bf16[32,2048]{1,0:T(8,128)(2,1)S(1)}, u32[]{:S(2)}, u32[]{:S(2)}) %collective-permute-start) | collective-permute-done | bytes 131104 | tf_op jit(solution)/shard_map/ppermute | solution.py:318
  54.4 2.7 %shard_map.147 = (bf16[32,2048]{1,0:T(8,128)(2,1)S(1)}, f32[32,2048]{1,0:T(8,128)S(1)}, f32[32,2048]{1,0:T(8,128)S(1)}, f32[32,16]{1,0:T(8,128)S(1)}) custom-call(bf16[128,2048]{1,0:T(8,128)(2,1)S(1)} %bitcast.48, bf16[128,2048]{1,0:T(8,128)(2,1)S(1)} %bitcast.37, bf16[128,2048]{1,0:T(8,128)(2,1)S(1)} %bitcast.41, bf16[128,2048]{1,0:T(8,128)(2,1)S(1)} %bitcast.49, ...), custom_call_target="tpu_custom_call" | custom-call | flops 100000000 | bytes 2771072 | tf_op jit(solution)/shard_map/pallas_call | solution.py:23
  59.3 3.0 %collective-permute-start.7 = (bf16[2,4,16,384]{3,2,1,0:T(8,128)(2,1)}, bf16[2,4,16,384]{3,2,1,0:T(8,128)(2,1)}, u32[]{:S(2)}, u32[]{:S(2)}) collective-permute-start(bf16[2,4,16,384]{3,2,1,0:T(8,128)(2,1)} %pad_maximum_fusion.7), channel_id=1, source_target_pairs={{0,8},{4,12},{8,0},{12,4},{16,24},{20,28},{24,16},{28,20},{1,9},{5... | collective-permute-start | bytes 294920 | tf_op jit(solution)/shard_map/ppermute | solution.py:318
  67.9 7.7 %all-to-all-start.2 = ((bf16[8,32,2048]{2,1,0:T(8,128)(2,1)}), bf16[8,32,2048]{2,1,0:T(8,128)(2,1)}, u32[]{:S(2)}, u32[]{:S(2)}) async-start(bf16[8,32,2048]{2,1,0:T(8,128)(2,1)} %copy-done.14), calls=%async_computation.2 | async-start | bytes 2097152 | tf_op jit(solution)/shard_map/all_to_all | solution.py:55
  77.9 4.3 %collective-permute-start.8 = (bf16[4,4,16,384]{3,2,1,0:T(8,128)(2,1)S(1)}, bf16[4,4,16,384]{3,2,1,0:T(8,128)(2,1)S(1)}, u32[]{:S(2)}, u32[]{:S(2)}) collective-permute-start(bf16[4,4,16,384]{3,2,1,0:T(8,128)(2,1)S(1)} %pad_maximum_fusion.6), channel_id=1, source_target_pairs={{0,16},{4,20},{8,24},{12,28},{16,0},{20,4},{24,8},{28,12},{1,17},{... | collective-permute-start | bytes 589832 | tf_op jit(solution)/shard_map/ppermute | solution.py:318
  82.2 7.8 %collective-permute-done.8 = bf16[4,4,16,384]{3,2,1,0:T(8,128)(2,1)S(1)} collective-permute-done((bf16[4,4,16,384]{3,2,1,0:T(8,128)(2,1)S(1)}, bf16[4,4,16,384]{3,2,1,0:T(8,128)(2,1)S(1)}, u32[]{:S(2)}, u32[]{:S(2)}) %collective-permute-start.8) | collective-permute-done | bytes 196640 | tf_op jit(solution)/shard_map/ppermute | solution.py:318
  91.0 2.8 %collective-permute-start.10 = (bf16[8,4,16,384]{3,2,1,0:T(8,128)(2,1)S(1)}, bf16[8,4,16,384]{3,2,1,0:T(8,128)(2,1)S(1)}, u32[]{:S(2)}, u32[]{:S(2)}) collective-permute-start(bf16[8,4,16,384]{3,2,1,0:T(8,128)(2,1)S(1)} %pad_maximum_fusion.2.w0), channel_id=1, source_target_pairs={{0,128},{64,192},{128,0},{192,64},{1,129},{65,193},{129,1},{193,65... | collective-permute-start | bytes 1179656 | tf_op jit(solution)/shard_map/ppermute | solution.py:323
  97.3 4.7 %collective-permute-done.10.w2 = bf16[8,4,16,384]{3,2,1,0:T(8,128)(2,1)S(1)} collective-permute-done((bf16[8,4,16,384]{3,2,1,0:T(8,128)(2,1)S(1)}, bf16[8,4,16,384]{3,2,1,0:T(8,128)(2,1)S(1)}, u32[]{:S(2)}, u32[]{:S(2)}) %collective-permute-start.10) | collective-permute-done | bytes 393248 | tf_op jit(solution)/shard_map/ppermute | solution.py:323
  102.8 8.2 %collective-permute-done.11.w3 = bf16[8,4,16,384]{3,2,1,0:T(8,128)(2,1)S(1)} collective-permute-done((bf16[8,4,16,384]{3,2,1,0:T(8,128)(2,1)S(1)}, bf16[8,4,16,384]{3,2,1,0:T(8,128)(2,1)S(1)}, u32[]{:S(2)}, u32[]{:S(2)}) %collective-permute-start.11) | collective-permute-done | bytes 393248 | tf_op jit(solution)/shard_map/ppermute | solution.py:323
  118.0 4.5 %shard_map.151 = (bf16[8,32,2048]{2,1,0:T(8,128)(2,1)S(1)}, bf16[512,384]{1,0:T(8,128)(2,1)S(1)}, bf16[512,384]{1,0:T(8,128)(2,1)S(1)}, bf16[512,384]{1,0:T(8,128)(2,1)S(1)}, bf16[512,384]{1,0:T(8,128)(2,1)S(1)}) custom-call(s32[5]{0:T(128)S(1)} %stack.65.ids, bf16[8,32,2048]{2,1,0:T(8,128)(2,1)} %all-to-all-done.2.rows, ...), custom_call_target="tpu_custom_call" | custom-call | flops 2000000000 | bytes 6291476 | tf_op jit(solution)/shard_map/pallas_call | solution.py:23
  126.5 6.1 %all-to-all-start.3 = ((bf16[8,32,2048]{2,1,0:T(8,128)(2,1)}), bf16[8,32,2048]{2,1,0:T(8,128)(2,1)}, u32[]{:S(2)}, u32[]{:S(2)}) async-start(bf16[8,32,2048]{2,1,0:T(8,128)(2,1)} %copy-done.15), calls=%async_computation.3 | async-start | bytes 2097152 | tf_op jit(solution)/shard_map/all_to_all | solution.py:55
  133.8 2.4 %collective-permute-start.21 = (bf16[512,384]{1,0:T(8,128)(2,1)}, bf16[512,384]{1,0:T(8,128)(2,1)S(1)}, u32[]{:S(2)}, u32[]{:S(2)}) collective-permute-start(bf16[512,384]{1,0:T(8,128)(2,1)} %copy-done.45), channel_id=1, source_target_pairs={{0,128},{64,192},{128,0},{192,64},{1,129},{65,193},{129,1},{193,65... | collective-permute-start | bytes 1179656 | tf_op jit(solution)/shard_map/ppermute | solution.py:323
  138.0 6.9 %collective-permute-done.20.p1 = bf16[512,384]{1,0:T(8,128)(2,1)S(1)} collective-permute-done((bf16[512,384]{1,0:T(8,128)(2,1)}, bf16[512,384]{1,0:T(8,128)(2,1)S(1)}, u32[]{:S(2)}, u32[]{:S(2)}) %collective-permute-start.20) | collective-permute-done | bytes 393248 | tf_op jit(solution)/shard_map/ppermute | solution.py:323
  144.9 9.2 %collective-permute-done.21.p2 = bf16[512,384]{1,0:T(8,128)(2,1)S(1)} collective-permute-done((bf16[512,384]{1,0:T(8,128)(2,1)}, bf16[512,384]{1,0:T(8,128)(2,1)S(1)}, u32[]{:S(2)}, u32[]{:S(2)}) %collective-permute-start.21) | collective-permute-done | bytes 393248 | tf_op jit(solution)/shard_map/ppermute | solution.py:323
  156.0 7.2 %all-to-all-start.4 = ((bf16[8,2,32,384]{3,2,1,0:T(8,128)(2,1)}), bf16[8,2,32,384]{3,2,1,0:T(8,128)(2,1)}, u32[]{:S(2)}, u32[]{:S(2)}) async-start(bf16[8,2,32,384]{3,2,1,0:T(8,128)(2,1)} %copy-done.7), calls=%async_computation.4 | async-start | bytes 786432 | tf_op jit(solution)/shard_map/all_to_all | solution.py:55
  171.0 2.3 %collective-permute-start.18 = (bf16[2,32,2048]{2,1,0:T(8,128)(2,1)S(1)}, bf16[2,32,2048]{2,1,0:T(8,128)(2,1)}, u32[]{:S(2)}, u32[]{:S(2)}) collective-permute-start(bf16[2,32,2048]{2,1,0:T(8,128)(2,1)S(1)} %pad_maximum_fusion.5.q0), channel_id=1, source_target_pairs={{0,128},{64,192},{128,0},{192,64},{1,129},{65,193},{129,1},{193,65... | collective-permute-start | bytes 786440 | tf_op jit(solution)/shard_map/ppermute | solution.py:323
  177.5 2.1 %collective-permute-start.15 = (bf16[2,32,2048]{2,1,0:T(8,128)(2,1)}, bf16[2,32,2048]{2,1,0:T(8,128)(2,1)}, u32[]{:S(2)}, u32[]{:S(2)}) collective-permute-start(bf16[2,32,2048]{2,1,0:T(8,128)(2,1)} %pad_maximum_fusion.4.a0), channel_id=1, source_target_pairs={{0,192},{64,0},{128,64},{192,128},{1,193},{65,1},{129,65},{193,129... | collective-permute-start | bytes 786440 | tf_op jit(solution)/shard_map/ppermute | solution.py:323
  181.4 7.6 %all-to-all-start.5 = ((f32[4,16,384]{2,1,0:T(8,128)}), f32[4,16,384]{2,1,0:T(8,128)}, u32[]{:S(2)}, u32[]{:S(2)}) async-start(f32[4,16,384]{2,1,0:T(8,128)} %bitcast.51), calls=%async_computation.5 | async-start | bytes 196608 | tf_op jit(solution)/shard_map/all_to_all | solution.py:55
  194.1 5.7 %shard_map.153 = bf16[128,2048]{1,0:T(8,128)(2,1)} custom-call(bf16[32,2048]{1,0:T(8,128)(2,1)S(1)} %copy-done.9, bf16[128,2048]{1,0:T(8,128)(2,1)S(1)} %bitcast.39, bf16[128,2048]{1,0:T(8,128)(2,1)S(1)} %bitcast.42, s32[1,32]{1,0:T(1,128)S(1)} %bitcast.59, f32[32,16]{1,0:T(8,128)S(1)} %get-tuple-element.38.cm, f32[16,128]{1,0:T(8,128)S(1)} %get-tuple-element.33.cum, ...), custom_call_target="tpu_custom_call" | custom-call | flops 100000000 | bytes 2771072 | tf_op jit(solution)/shard_map/pallas_call | solution.py:23
  205.2 4.9 %shard_map.155 = (bf16[128,2048]{1,0:T(8,128)(2,1)}, bf16[128,2048]{1,0:T(8,128)(2,1)}) custom-call(bf16[2,32,2048]{2,1,0:T(8,128)(2,1)} %pad_maximum_fusion.4.a0, bf16[2,32,2048]{2,1,0:T(8,128)(2,1)} %collective-permute-done.13.a1, bf16[2,32,2048]{2,1,0:T(8,128)(2,1)} %collective-permute-done.14.a2, bf16[2,32,2048]{2,1,0:T(8,128)(2,1)} %collective-permute-done.15.a3, ...), custom_call_target="tpu_custom_call" | custom-call | flops 100000000 | bytes 6815744 | tf_op jit(solution)/shard_map/pallas_call | solution.py:23
  (177 shorter events, 74.0 us)
Async XLA Ops:
  7.1 20.8 %all-to-all-start = ((bf16[8,528,128]{2,1,0:T(8,128)(2,1)}), bf16[8,528,128]{2,1,0:T(8,128)(2,1)S(1)}, u32[]{:S(2)}, u32[]{:S(2)}) async-start(bf16[8,528,128]{2,1,0:T(8,128)(2,1)} %copy-done.10), calls=%async_computation | async-start | bytes 2162688 | tf_op jit(solution)/shard_map/all_to_all | solution.py:55
  29.8 32.5 %all-to-all-start.1 = ((bf16[8,512,128]{2,1,0:T(8,128)(2,1)}), bf16[8,512,128]{2,1,0:T(8,128)(2,1)S(1)}, u32[]{:S(2)}, u32[]{:S(2)}) async-start(bf16[8,512,128]{2,1,0:T(8,128)(2,1)} %copy-done.4), calls=%async_computation.1 | async-start | bytes 2097152 | tf_op jit(solution)/shard_map/all_to_all | solution.py:55
  36.6 13.6 %collective-permute-start = (bf16[32,2048]{1,0:T(8,128)(2,1)S(1)}, bf16[32,2048]{1,0:T(8,128)(2,1)S(1)}, u32[]{:S(2)}, u32[]{:S(2)}) collective-permute-start(bf16[32,2048]{1,0:T(8,128)(2,1)S(1)} %get-tuple-element.42), channel_id=1, source_target_pairs={{0,1},{1,0},{2,3},{3,2},{4,5},{5,4},{6,7},{7,6},{8,9},{9,8},{10,11... | collective-permute-start | bytes 393224 | tf_op jit(solution)/shard_map/ppermute | solution.py:318
  39.1 12.5 %collective-permute-start.3 = (bf16[16,384]{1,0:T(8,128)(2,1)S(1)}, bf16[16,384]{1,0:T(8,128)(2,1)S(1)}, u32[]{:S(2)}, u32[]{:S(2)}) collective-permute-start(bf16[16,384]{1,0:T(8,128)(2,1)S(1)} %get-tuple-element.44), channel_id=1, source_target_pairs={{0,2},{2,0},{32,34},{34,32},{1,3},{3,1},{33,35},{35,33},{4,6},{6,4... | collective-permute-start | bytes 36872 | tf_op jit(solution)/shard_map/ppermute | solution.py:351
  50.9 24.7 %collective-permute-start.1 = (bf16[2,32,2048]{2,1,0:T(8,128)(2,1)}, bf16[2,32,2048]{2,1,0:T(8,128)(2,1)}, u32[]{:S(2)}, u32[]{:S(2)}) collective-permute-start(bf16[2,32,2048]{2,1,0:T(8,128)(2,1)} %pad_maximum_fusion.3), channel_id=1, source_target_pairs={{0,32},{32,0},{1,33},{33,1},{2,34},{34,2},{3,35},{35,3},{4,36},{36... | collective-permute-start | bytes 786440 | tf_op jit(solution)/shard_map/ppermute | solution.py:318
  59.3 17.6 %collective-permute-start.7 = (bf16[2,4,16,384]{3,2,1,0:T(8,128)(2,1)}, bf16[2,4,16,384]{3,2,1,0:T(8,128)(2,1)}, u32[]{:S(2)}, u32[]{:S(2)}) collective-permute-start(bf16[2,4,16,384]{3,2,1,0:T(8,128)(2,1)} %pad_maximum_fusion.7), channel_id=1, source_target_pairs={{0,8},{4,12},{8,0},{12,4},{16,24},{20,28},{24,16},{28,20},{1,9},{5... | collective-permute-start | bytes 294920 | tf_op jit(solution)/shard_map/ppermute | solution.py:318
  67.9 44.9 %all-to-all-start.2 = ((bf16[8,32,2048]{2,1,0:T(8,128)(2,1)}), bf16[8,32,2048]{2,1,0:T(8,128)(2,1)}, u32[]{:S(2)}, u32[]{:S(2)}) async-start(bf16[8,32,2048]{2,1,0:T(8,128)(2,1)} %copy-done.14), calls=%async_computation.2 | async-start | bytes 2097152 | tf_op jit(solution)/shard_map/all_to_all | solution.py:55
  76.7 18.5 %collective-permute-start.2 = (bf16[4,32,2048]{2,1,0:T(8,128)(2,1)S(1)}, bf16[4,32,2048]{2,1,0:T(8,128)(2,1)S(1)}, u32[]{:S(2)}, u32[]{:S(2)}) collective-permute-start(bf16[4,32,2048]{2,1,0:T(8,128)(2,1)S(1)} %pad_maximum_fusion.1), channel_id=1, source_target_pairs={{0,2},{2,0},{1,3},{3,1},{4,6},{6,4},{5,7},{7,5},{8,10},{10,8},{9,1... | collective-permute-start | bytes 1572872 | tf_op jit(solution)/shard_map/ppermute | solution.py:318
  77.9 12.1 %collective-permute-start.8 = (bf16[4,4,16,384]{3,2,1,0:T(8,128)(2,1)S(1)}, bf16[4,4,16,384]{3,2,1,0:T(8,128)(2,1)S(1)}, u32[]{:S(2)}, u32[]{:S(2)}) collective-permute-start(bf16[4,4,16,384]{3,2,1,0:T(8,128)(2,1)S(1)} %pad_maximum_fusion.6), channel_id=1, source_target_pairs={{0,16},{4,20},{8,24},{12,28},{16,0},{20,4},{24,8},{28,12},{1,17},{... | collective-permute-start | bytes 589832 | tf_op jit(solution)/shard_map/ppermute | solution.py:318
  91.0 11.0 %collective-permute-start.10 = (bf16[8,4,16,384]{3,2,1,0:T(8,128)(2,1)S(1)}, bf16[8,4,16,384]{3,2,1,0:T(8,128)(2,1)S(1)}, u32[]{:S(2)}, u32[]{:S(2)}) collective-permute-start(bf16[8,4,16,384]{3,2,1,0:T(8,128)(2,1)S(1)} %pad_maximum_fusion.2.w0), channel_id=1, source_target_pairs={{0,128},{64,192},{128,0},{192,64},{1,129},{65,193},{129,1},{193,65... | collective-permute-start | bytes 1179656 | tf_op jit(solution)/shard_map/ppermute | solution.py:323
  93.8 17.2 %collective-permute-start.11 = (bf16[8,4,16,384]{3,2,1,0:T(8,128)(2,1)S(1)}, bf16[8,4,16,384]{3,2,1,0:T(8,128)(2,1)S(1)}, u32[]{:S(2)}, u32[]{:S(2)}) collective-permute-start(bf16[8,4,16,384]{3,2,1,0:T(8,128)(2,1)S(1)} %pad_maximum_fusion.2.w0), channel_id=1, source_target_pairs={{0,192},{64,0},{128,64},{192,128},{1,193},{65,1},{129,65},{193,129... | collective-permute-start | bytes 1179656 | tf_op jit(solution)/shard_map/ppermute | solution.py:323
  94.6 17.4 %collective-permute-start.9 = (bf16[8,4,16,384]{3,2,1,0:T(8,128)(2,1)S(1)}, bf16[8,4,16,384]{3,2,1,0:T(8,128)(2,1)S(1)}, u32[]{:S(2)}, u32[]{:S(2)}) collective-permute-start(bf16[8,4,16,384]{3,2,1,0:T(8,128)(2,1)S(1)} %pad_maximum_fusion.2.w0), channel_id=1, source_target_pairs={{0,64},{64,128},{128,192},{192,0},{1,65},{65,129},{129,193},{193,1... | collective-permute-start | bytes 1179656 | tf_op jit(solution)/shard_map/ppermute | solution.py:323
  126.5 29.5 %all-to-all-start.3 = ((bf16[8,32,2048]{2,1,0:T(8,128)(2,1)}), bf16[8,32,2048]{2,1,0:T(8,128)(2,1)}, u32[]{:S(2)}, u32[]{:S(2)}) async-start(bf16[8,32,2048]{2,1,0:T(8,128)(2,1)} %copy-done.15), calls=%async_computation.3 | async-start | bytes 2097152 | tf_op jit(solution)/shard_map/all_to_all | solution.py:55
  132.6 12.3 %collective-permute-start.20 = (bf16[512,384]{1,0:T(8,128)(2,1)}, bf16[512,384]{1,0:T(8,128)(2,1)S(1)}, u32[]{:S(2)}, u32[]{:S(2)}) collective-permute-start(bf16[512,384]{1,0:T(8,128)(2,1)} %copy-done.48), channel_id=1, source_target_pairs={{0,64},{64,128},{128,192},{192,0},{1,65},{65,129},{129,193},{193,1... | collective-permute-start | bytes 1179656 | tf_op jit(solution)/shard_map/ppermute | solution.py:323
  133.8 20.3 %collective-permute-start.21 = (bf16[512,384]{1,0:T(8,128)(2,1)}, bf16[512,384]{1,0:T(8,128)(2,1)S(1)}, u32[]{:S(2)}, u32[]{:S(2)}) collective-permute-start(bf16[512,384]{1,0:T(8,128)(2,1)} %copy-done.45), channel_id=1, source_target_pairs={{0,128},{64,192},{128,0},{192,64},{1,129},{65,193},{129,1},{193,65... | collective-permute-start | bytes 1179656 | tf_op jit(solution)/shard_map/ppermute | solution.py:323
  136.2 17.9 %collective-permute-start.22 = (bf16[512,384]{1,0:T(8,128)(2,1)}, bf16[512,384]{1,0:T(8,128)(2,1)S(1)}, u32[]{:S(2)}, u32[]{:S(2)}) collective-permute-start(bf16[512,384]{1,0:T(8,128)(2,1)} %copy-done.42), channel_id=1, source_target_pairs={{0,192},{64,0},{128,64},{192,128},{1,193},{65,1},{129,65},{193,129... | collective-permute-start | bytes 1179656 | tf_op jit(solution)/shard_map/ppermute | solution.py:323
  136.6 31.7 %collective-permute-start.16 = (bf16[32,2048]{1,0:T(8,128)(2,1)S(1)}, bf16[32,2048]{1,0:T(8,128)(2,1)}, u32[]{:S(2)}, u32[]{:S(2)}) collective-permute-start(bf16[32,2048]{1,0:T(8,128)(2,1)S(1)} %get-tuple-element.35.qm), channel_id=1, source_target_pairs={{0,32},{32,0},{1,33},{33,1},{2,34},{34,2},{3,35},{35,3},{4,36},{36... | collective-permute-start | bytes 393224 | tf_op jit(solution)/shard_map/ppermute | solution.py:318
  156.0 23.6 %all-to-all-start.4 = ((bf16[8,2,32,384]{3,2,1,0:T(8,128)(2,1)}), bf16[8,2,32,384]{3,2,1,0:T(8,128)(2,1)}, u32[]{:S(2)}, u32[]{:S(2)}) async-start(bf16[8,2,32,384]{3,2,1,0:T(8,128)(2,1)} %copy-done.7), calls=%async_computation.4 | async-start | bytes 786432 | tf_op jit(solution)/shard_map/all_to_all | solution.py:55
  171.0 18.0 %collective-permute-start.18 = (bf16[2,32,2048]{2,1,0:T(8,128)(2,1)S(1)}, bf16[2,32,2048]{2,1,0:T(8,128)(2,1)}, u32[]{:S(2)}, u32[]{:S(2)}) collective-permute-start(bf16[2,32,2048]{2,1,0:T(8,128)(2,1)S(1)} %pad_maximum_fusion.5.q0), channel_id=1, source_target_pairs={{0,128},{64,192},{128,0},{192,64},{1,129},{65,193},{129,1},{193,65... | collective-permute-start | bytes 786440 | tf_op jit(solution)/shard_map/ppermute | solution.py:323
  173.3 15.7 %collective-permute-start.19 = (bf16[2,32,2048]{2,1,0:T(8,128)(2,1)S(1)}, bf16[2,32,2048]{2,1,0:T(8,128)(2,1)}, u32[]{:S(2)}, u32[]{:S(2)}) collective-permute-start(bf16[2,32,2048]{2,1,0:T(8,128)(2,1)S(1)} %pad_maximum_fusion.5.q0), channel_id=1, source_target_pairs={{0,192},{64,0},{128,64},{192,128},{1,193},{65,1},{129,65},{193,129... | collective-permute-start | bytes 786440 | tf_op jit(solution)/shard_map/ppermute | solution.py:323
  174.3 27.2 %collective-permute-start.13 = (bf16[2,32,2048]{2,1,0:T(8,128)(2,1)}, bf16[2,32,2048]{2,1,0:T(8,128)(2,1)}, u32[]{:S(2)}, u32[]{:S(2)}) collective-permute-start(bf16[2,32,2048]{2,1,0:T(8,128)(2,1)} %pad_maximum_fusion.4.a0), channel_id=1, source_target_pairs={{0,64},{64,128},{128,192},{192,0},{1,65},{65,129},{129,193},{193,1... | collective-permute-start | bytes 786440 | tf_op jit(solution)/shard_map/ppermute | solution.py:323
  175.5 26.0 %collective-permute-start.14 = (bf16[2,32,2048]{2,1,0:T(8,128)(2,1)}, bf16[2,32,2048]{2,1,0:T(8,128)(2,1)}, u32[]{:S(2)}, u32[]{:S(2)}) collective-permute-start(bf16[2,32,2048]{2,1,0:T(8,128)(2,1)} %pad_maximum_fusion.4.a0), channel_id=1, source_target_pairs={{0,128},{64,192},{128,0},{192,64},{1,129},{65,193},{129,1},{193,65... | collective-permute-start | bytes 786440 | tf_op jit(solution)/shard_map/ppermute | solution.py:323
  177.5 23.9 %collective-permute-start.15 = (bf16[2,32,2048]{2,1,0:T(8,128)(2,1)}, bf16[2,32,2048]{2,1,0:T(8,128)(2,1)}, u32[]{:S(2)}, u32[]{:S(2)}) collective-permute-start(bf16[2,32,2048]{2,1,0:T(8,128)(2,1)} %pad_maximum_fusion.4.a0), channel_id=1, source_target_pairs={{0,192},{64,0},{128,64},{192,128},{1,193},{65,1},{129,65},{193,129... | collective-permute-start | bytes 786440 | tf_op jit(solution)/shard_map/ppermute | solution.py:323
  181.4 18.5 %all-to-all-start.5 = ((f32[4,16,384]{2,1,0:T(8,128)}), f32[4,16,384]{2,1,0:T(8,128)}, u32[]{:S(2)}, u32[]{:S(2)}) async-start(f32[4,16,384]{2,1,0:T(8,128)} %bitcast.51), calls=%async_computation.5 | async-start | bytes 196608 | tf_op jit(solution)/shard_map/all_to_all | solution.py:55
  (64 other events, 307.1 us)

commit v3 on v2

--- a/solution.py
+++ b/solution.py
@@ -19,13 +19,15 @@
 def call(body, outs, *args, flops=10**8, scalar=False, scratch=()):
     shapes = [jax.ShapeDtypeStruct(s, d) for s, d in outs]
     moved = sum(a.size * a.dtype.itemsize for a in (*args, *shapes))
-    spaces = [pltpu.SMEM if scalar and k == 0 else pltpu.VMEM for k in range(len(args))]
+    in_specs = [pl.BlockSpec()] * len(args)
+    if scalar:
+        in_specs[0] = pl.BlockSpec(memory_space=pltpu.SMEM)
     result = pl.pallas_call(
         body,
         out_shape=shapes,
-        in_specs=[pl.BlockSpec(memory_space=m) for m in spaces],
+        in_specs=in_specs,
         scratch_shapes=list(scratch),
-        compiler_params=pltpu.CompilerParams(vmem_limit_bytes=20 << 20),
+        compiler_params=pltpu.CompilerParams(vmem_limit_bytes=56 << 20),
         cost_estimate=pl.CostEstimate(flops=flops, bytes_accessed=moved, transcendentals=0),
     )(*args)
     return result
@@ -92,7 +94,7 @@
         down[:, head(b)] = jnp.where(low, pltpu.roll(x, 64, 1), y)
 
 
-def states_body(ld, key, value, places, out, cum_out, cum_t_out):
+def states_body(ld, key, value, mask, out, cum_out, cum_t_out):
     rows, cols = iota((HD, HD), 0), iota((HD, HD), 1)
     ldv = ld[...]
     cum = nn(ldv, (rows <= cols).astype(F32), precision=HIGH)
@@ -109,7 +111,10 @@
         g, at = h // 2, (h % 2) * HD
         out[g, at : at + HD, :] = tn(kf, v).astype(BF16)
         out[g, 256 + at : 256 + at + HD, :] = tn(kb, v).astype(BF16)
-    chosen = nn(cum, (rows == places[...]).astype(F32), precision=HIGH)
+    repeat = (iota((32, HD), 0) == iota((32, HD), 1) % 32).astype(BF16)
+    places = nn(mask[...].astype(F32).astype(BF16), repeat).astype(jnp.int32)
+    places = jnp.where(iota((1, HD), 1) < 96, places, HD - 1)
+    chosen = nn(cum, (rows == places).astype(F32), precision=HIGH)
     hi = chosen.astype(BF16).astype(F32)
     mid = (chosen - hi).astype(BF16).astype(F32)
     low = (chosen - hi - mid).astype(BF16).astype(F32)
@@ -192,7 +197,7 @@
             routed_out[k, :, head(h)] = routed
 
 
-def expert_body(ids, rows, grads, w0, w1, w2, w3, z_out, d0, d1, d2, d3, w_ref, g_ref):
+def expert_body(ids, rows, g1, g2, g3, g4, w0, w1, w2, w3, z_out, d0, d1, d2, d3, w_ref, g_ref):
     nz, unit = w0.shape[0], w0.shape[2]
     for k, piece in enumerate((w0, w1, w2, w3)):
         y = (ids[Y] + 4 - k) % 4
@@ -201,9 +206,12 @@
                 x = ids[XL] ^ (cs // 2)
                 at = (((y * 2 + x) * nz + (ids[Z] ^ zs)) * 2 + (ids[C] ^ (cs % 2))) * unit
                 w_ref[pl.ds(pl.multiple_of(at, unit), unit), :] = piece[zs, cs]
-    for k in range(8):
-        slot = ((k % 2) ^ ids[E]) + 2 * ((k // 4) ^ ids[XL]) + 4 * ((k // 2 % 2) ^ ids[C])
-        g_ref[k] = grads[slot]
+    slot = 0
+    for piece in (g1, g2, g3, g4):
+        for j in range(piece.shape[0]):
+            there = 4 * (ids[XL] ^ (slot // 2 % 2)) + 2 * (ids[C] ^ (slot // 4)) + (ids[E] ^ (slot % 2))
+            g_ref[there] = piece[j]
+            slot += 1
     width = HEADS * HD
     r = rows[...].reshape(256, width)
     g = g_ref[...].reshape(256, width)
@@ -323,6 +331,10 @@
     return lax.ppermute(x, "y", [(i, (i + k) % n) for i in range(n)])
 
 
+def after(first, then):
+    return lax.optimization_barrier((first, then))
+
+
 def along_y(x):
     return [x] + [turn(x, k) for k in range(1, 4)]
 
@@ -338,7 +350,6 @@
     ny, nx, nz, nc = (lax.axis_size(a) for a in ("y", "xl", "z", "c"))
     shard = up.shape[0]
     ids = jnp.stack([lax.axis_index(a) for a in ("y", "xl", "z", "c", "e")]).astype(jnp.int32)
-    places = jnp.concatenate((mask, mask, mask, jnp.full_like(mask, HD - 1)), axis=1)
 
     prepared = call(
         prepare_body,
@@ -347,14 +358,16 @@
         scalar=True,
         scratch=[pltpu.VMEM((4, shard, 384), BF16)],
     )
+    prepared, ld = after(prepared, ld)
     w = [prepared[0]] + [
         lax.ppermute(prepared[k], ("xl", "c"), [(i, i ^ k) for i in range(4)]) for k in range(1, 4)
     ]
-    grads = jnp.stack((prepared[4], trade(prepared[5], "e")))
+    own = prepared[4][None]
+    from_e = trade(prepared[5][None], "e")
     states, cum, cum_t = call(
         states_body,
         [((8, 528, HD), BF16), ((HEADS, HD), F32), ((HD, HEADS), F32)],
-        ld, key, value, places,
+        ld, key, value, mask,
     )
     parts = exchange(states, SEQ)
     qm, rm, inner, cm = call(
@@ -362,15 +375,19 @@
         [((32, width), BF16), ((32, width), F32), ((32, width), F32), ((32, HEADS), F32)],
         query, key, value, residual, mask, cum, cum_t,
     )
+    w = jnp.stack(w)[None]
+    (w, from_e, qm), parts = after((w, from_e, qm), parts)
     [carries] = call(carry_body, [((8, 512, HD), BF16)], ids, parts, scalar=True)
     carried = exchange(carries, SEQ)
-    grads = jnp.concatenate((grads, trade(grads, "xl")))
-    grads = jnp.concatenate((grads, trade(grads, "c")))
-    w = jnp.stack(w)[None]
+    two = jnp.concatenate((own, from_e))
+    from_x = trade(two, "xl")
+    q_two = jnp.stack((qm, trade(qm, "xl")))
     bit = 1
     while bit < nz:
         w = jnp.concatenate((w, trade(w, "z", bit)))
         bit *= 2
+    (w, from_x, q_two), carried = after((w, from_x, q_two), carried)
+    from_c = trade(jnp.concatenate((two, from_x)), "c")
     routed8, normed, normalized, stats = call(
         rows_body,
         [((8, 32, width), BF16), ((32, width), F32), ((32, width), F32), ((32, HD), F32)],
@@ -381,21 +398,24 @@
     z_send, *dw = call(
         expert_body,
         [((8, 32, width), BF16)] + [((width // ny, 384), BF16)] * 4,
-        ids, rows, grads, *weights,
+        ids, rows, own, from_e, from_x, from_c, *weights,
         scalar=True,
         scratch=[pltpu.VMEM((width, 384), BF16), pltpu.VMEM((8, 32, width), BF16)],
         flops=2 * 10**9,
     )
+    q_two, dw = after(q_two, dw)
+    queries = along_y(q_two)
     z_parts = exchange(z_send, GRP)
-    queries = along_sequence(qm)
     d1 = [dw[0]] + [turn(dw[k], k) for k in range(1, 4)]
+    (queries, d1), z_parts = after((queries, d1), z_parts)
+    [da] = call(grads_body, [((32, width), BF16)], z_parts, cot, normed, normalized, stats)
+    d1, da = after(d1, da)
     decay, scores = call(
         scores_body,
         [((HEADS, HD, 256), F32), ((HEADS, HD, 256), BF16)],
         ids, parts, *queries, key, cum_t,
         scalar=True,
     )
-    [da] = call(grads_body, [((32, width), BF16)], z_parts, cot, normed, normalized, stats)
     das = along_sequence(da)
     [d2] = call(sum_y_body, [((nz, nx, nc * shard, 384), BF16)], *d1)
     d3 = exchange(d2, "z")

time: 212 us -> 200 us (0.943)
  local copies, waits for them, and re-layouts: 36.7 us -> 8.61 us
  Pallas kernels: 29.6 us -> 50 us
  starting transfers between devices: 73.8 us -> 83.2 us
  other arithmetic: 8.95 us -> 0.24 us
  waiting for transfers between devices: 60.2 us -> 55.9 us
    unnamed x118 -> x64, local copies, waits for them, and re-layouts: 36.6 us -> 7.93 us
    pallas_call x13, Pallas kernels: 29.6 us -> 50 us  [call(): pl.pallas_call(body, out_shape=shapes, in_specs=in_specs, scratch_shapes=...]
    all_to_all x6, waiting for transfers between devices: 14.8 us -> 5.84 us  [exchange(): return lax.all_to_all(x, axes, split_axis=0, concat_axis=0, tiled=True)]
    ppermute x12, starting transfers between devices: 16.6 us -> 24.6 us  [turn(): return lax.ppermute(x, 'y', [(i, (i + k) % n) for i in range(n)])]
    ppermute x8, waiting for transfers between devices: 15.4 us -> 7.86 us  [trade(): return lax.ppermute(x, axis, [(i, i ^ bit) for i in range(n)])]
    ppermute x3, waiting for transfers between devices: 0.01 us -> 7.32 us  [local(): lax.ppermute(prepared[k], ('xl', 'c'), [(i, i ^ k) for i in range(4)])]
    ppermute x12, waiting for transfers between devices: 30 us -> 34.9 us  [turn(): return lax.ppermute(x, 'y', [(i, (i + k) % n) for i in range(n)])]
    concatenate x3 -> x2, other arithmetic: 3.96 us -> 0.08 us  [the longest x1 0.05 us: local(): from_c = trade(jnp.concatenate((two, from_x)), 'c')]
  transfers between devices with their start and end apart: 29 -> 29, of which waited for: 9 -> 13; matrix products, arithmetic and copies ran while one was open for 4% -> 0% of each run, Pallas kernels for 8% -> 12%
where the time goes in v3:
time: 200 us; the launch traced here: 199 us
  starting transfers between devices  83.2 us (42%)
  waiting for transfers between devices  55.9 us (28%)
  Pallas kernels  50 us (25%)
  local copies, waits for them, and re-layouts  8.61 us (4%)
    pallas_call x13, Pallas kernels, call(): pl.pallas_call(body, out_shape=shapes, in_specs=in_specs, scratch_shapes=...  50 us
    all_to_all x6, starting transfers between devices, exchange(): return lax.all_to_all(x, axes, split_axis=0, concat_axis=0, tiled=True)  36.9 us
    ppermute x12, waiting for transfers between devices, turn(): return lax.ppermute(x, 'y', [(i, (i + k) % n) for i in range(n)])  34.9 us
    ppermute x12, starting transfers between devices, turn(): return lax.ppermute(x, 'y', [(i, (i + k) % n) for i in range(n)])  24.6 us
    ppermute x8, starting transfers between devices, trade(): return lax.ppermute(x, axis, [(i, i ^ bit) for i in range(n)])  18.7 us
    unnamed x64, local copies, waits for them, and re-layouts  7.93 us
    ppermute x8, waiting for transfers between devices, trade(): return lax.ppermute(x, axis, [(i, i ^ bit) for i in range(n)])  7.86 us
    ppermute x3, waiting for transfers between devices, local(): lax.ppermute(prepared[k], ('xl', 'c'), [(i, i ^ k) for i in range(4)])  7.32 us
  transfers between devices with their start and end apart: 29, of which 13 were waited for; matrix products, arithmetic and copies ran while one was open for 0% of the time, Pallas kernels for 12%

profile of v3, /device:TPU:1, one launch (start us, length us, event | category | flops | bytes accessed | tf_op | source)
XLA Modules:
  0.0 198.9 jit_solution(7719556727272581116)
XLA Ops:
  3.4 4.2 %shard_map.147 = (bf16[8,528,128]{2,1,0:T(8,128)(2,1)}, f32[16,128]{1,0:T(8,128)}, f32[128,16]{1,0:T(8,128)}) custom-call(f32[16,128]{1,0:T(8,128)} %bitcast.59, bf16[128,2048]{1,0:T(8,128)(2,1)} %bitcast.34, bf16[128,2048]{1,0:T(8,128)(2,1)} %bitcast.38, s32[1,32]{1,0:T(1,128)} %bitcast.61), custom_call_target="tpu_custom_call" | custom-call | flops 100000000 | bytes 2154624 | tf_op jit(solution)/shard_map/pallas_call | solution.py:25
  7.6 6.1 %all-to-all-start = ((bf16[8,528,128]{2,1,0:T(8,128)(2,1)}), bf16[8,528,128]{2,1,0:T(8,128)(2,1)S(1)}, u32[]{:S(2)}, u32[]{:S(2)}) async-start(bf16[8,528,128]{2,1,0:T(8,128)(2,1)} %get-tuple-element.82), calls=%async_computation | async-start | bytes 2162688 | tf_op jit(solution)/shard_map/all_to_all | solution.py:57
  19.2 5.0 %shard_map.148 = (bf16[32,2048]{1,0:T(8,128)(2,1)}, f32[32,2048]{1,0:T(8,128)}, f32[32,2048]{1,0:T(8,128)}, f32[32,16]{1,0:T(8,128)}) custom-call(bf16[128,2048]{1,0:T(8,128)(2,1)} %bitcast.43, bf16[128,2048]{1,0:T(8,128)(2,1)} %bitcast.35, bf16[128,2048]{1,0:T(8,128)(2,1)} %bitcast.39, bf16[128,2048]{1,0:T(8,128)(2,1)} %bitcast.44, s32[1,32]{1,0:T(1,128)} %bitcast.62, ...), custom_call_target="tpu_custom_call" | custom-call | flops 100000000 | bytes 2771072 | tf_op jit(solution)/shard_map/pallas_call | solution.py:25
  24.2 5.6 %collective-permute-done.1 = bf16[16,384]{1,0:T(8,128)(2,1)S(1)} collective-permute-done((bf16[16,384]{1,0:T(8,128)(2,1)S(1)}, bf16[16,384]{1,0:T(8,128)(2,1)S(1)}, u32[]{:S(2)}, u32[]{:S(2)}) %collective-permute-start.1) | collective-permute-done | bytes 12320 | tf_op jit(solution)/shard_map/ppermute | solution.py:363
  35.2 4.1 %all-to-all-start.1 = ((bf16[8,512,128]{2,1,0:T(8,128)(2,1)}), bf16[8,512,128]{2,1,0:T(8,128)(2,1)S(1)}, u32[]{:S(2)}, u32[]{:S(2)}) async-start(bf16[8,512,128]{2,1,0:T(8,128)(2,1)} %shard_map.149), calls=%async_computation.1 | async-start | bytes 2097152 | tf_op jit(solution)/shard_map/all_to_all | solution.py:57
  42.4 3.1 %collective-permute-start.5 = (bf16[2,4,16,384]{3,2,1,0:T(8,128)(2,1)S(1)}, bf16[2,4,16,384]{3,2,1,0:T(8,128)(2,1)S(1)}, u32[]{:S(2)}, u32[]{:S(2)}) collective-permute-start(bf16[2,4,16,384]{3,2,1,0:T(8,128)(2,1)S(1)} %pad_maximum_fusion.6), channel_id=1, source_target_pairs={{0,8},{4,12},{8,0},{12,4},{16,24},{20,28},{24,16},{28,20},{1,9},{5... | collective-permute-start | bytes 294920 | tf_op jit(solution)/shard_map/ppermute | solution.py:326
  47.9 7.2 %collective-permute-start.6 = (bf16[4,4,16,384]{3,2,1,0:T(8,128)(2,1)S(1)}, bf16[4,4,16,384]{3,2,1,0:T(8,128)(2,1)S(1)}, u32[]{:S(2)}, u32[]{:S(2)}) collective-permute-start(bf16[4,4,16,384]{3,2,1,0:T(8,128)(2,1)S(1)} %pad_maximum_fusion.5), channel_id=1, source_target_pairs={{0,16},{4,20},{8,24},{12,28},{16,0},{20,4},{24,8},{28,12},{1,17},{... | collective-permute-start | bytes 589832 | tf_op jit(solution)/shard_map/ppermute | solution.py:326
  55.1 3.1 %collective-permute-done.6 = bf16[4,4,16,384]{3,2,1,0:T(8,128)(2,1)S(1)} collective-permute-done((bf16[4,4,16,384]{3,2,1,0:T(8,128)(2,1)S(1)}, bf16[4,4,16,384]{3,2,1,0:T(8,128)(2,1)S(1)}, u32[]{:S(2)}, u32[]{:S(2)}) %collective-permute-start.6) | collective-permute-done | bytes 196640 | tf_op jit(solution)/shard_map/ppermute | solution.py:326
  60.6 3.9 %shard_map.150 = (bf16[8,32,2048]{2,1,0:T(8,128)(2,1)}, f32[32,2048]{1,0:T(8,128)}, f32[32,2048]{1,0:T(8,128)}, f32[32,128]{1,0:T(8,128)}) custom-call(bf16[32,2048]{1,0:T(8,128)(2,1)} %get-tuple-element.86.qm, f32[32,2048]{1,0:T(8,128)} %get-tuple-element.89.rm, f32[32,2048]{1,0:T(8,128)} %get-tuple-element.90.inner, f32[32,16]{1,0:T(8,128)} %get-tuple-element.91.cm, ...), custom_call_target="tpu_custom_call" | custom-call | flops 100000000 | bytes 3303424 | tf_op jit(solution)/shard_map/pallas_call | solution.py:25
  64.4 11.0 %all-to-all-start.2 = ((bf16[8,32,2048]{2,1,0:T(8,128)(2,1)}), bf16[8,32,2048]{2,1,0:T(8,128)(2,1)S(1)}, u32[]{:S(2)}, u32[]{:S(2)}) async-start(bf16[8,32,2048]{2,1,0:T(8,128)(2,1)} %get-tuple-element.93), calls=%async_computation.2 | async-start | bytes 2097152 | tf_op jit(solution)/shard_map/all_to_all | solution.py:57
  75.6 3.0 %collective-permute-start.12 = (bf16[8,4,16,384]{3,2,1,0:T(8,128)(2,1)S(1)}, bf16[8,4,16,384]{3,2,1,0:T(8,128)(2,1)S(1)}, u32[]{:S(2)}, u32[]{:S(2)}) collective-permute-start(bf16[8,4,16,384]{3,2,1,0:T(8,128)(2,1)S(1)} %pad_maximum_fusion.1.w0), channel_id=1, source_target_pairs={{0,192},{64,0},{128,64},{192,128},{1,193},{65,1},{129,65},{193,129... | collective-permute-start | bytes 1179656 | tf_op jit(solution)/shard_map/ppermute | solution.py:331
  81.5 7.4 %collective-permute-done.12.w3 = bf16[8,4,16,384]{3,2,1,0:T(8,128)(2,1)S(1)} collective-permute-done((bf16[8,4,16,384]{3,2,1,0:T(8,128)(2,1)S(1)}, bf16[8,4,16,384]{3,2,1,0:T(8,128)(2,1)S(1)}, u32[]{:S(2)}, u32[]{:S(2)}) %collective-permute-start.12) | collective-permute-done | bytes 393248 | tf_op jit(solution)/shard_map/ppermute | solution.py:331
  90.1 9.5 %collective-permute-done.10.w1 = bf16[8,4,16,384]{3,2,1,0:T(8,128)(2,1)S(1)} collective-permute-done((bf16[8,4,16,384]{3,2,1,0:T(8,128)(2,1)S(1)}, bf16[8,4,16,384]{3,2,1,0:T(8,128)(2,1)S(1)}, u32[]{:S(2)}, u32[]{:S(2)}) %collective-permute-start.10) | collective-permute-done | bytes 393248 | tf_op jit(solution)/shard_map/ppermute | solution.py:331
  102.1 6.1 %shard_map.151 = (bf16[8,32,2048]{2,1,0:T(8,128)(2,1)}, bf16[512,384]{1,0:T(8,128)(2,1)}, bf16[512,384]{1,0:T(8,128)(2,1)}, bf16[512,384]{1,0:T(8,128)(2,1)}, bf16[512,384]{1,0:T(8,128)(2,1)}) custom-call(s32[5]{0:T(128)} %stack.56.ids, bf16[8,32,2048]{2,1,0:T(8,128)(2,1)} %copy-done.10, bf16[1,32,2048]{2,1,0:T(8,128)(2,1)} %bitcast.47, ...), custom_call_target="tpu_custom_call" | custom-call | flops 2000000000 | bytes 6291476 | tf_op jit(solution)/shard_map/pallas_call | solution.py:25
  108.2 5.2 %all-to-all-start.3 = ((bf16[8,32,2048]{2,1,0:T(8,128)(2,1)}), bf16[8,32,2048]{2,1,0:T(8,128)(2,1)S(1)}, u32[]{:S(2)}, u32[]{:S(2)}) async-start(bf16[8,32,2048]{2,1,0:T(8,128)(2,1)} %get-tuple-element.105), calls=%async_computation.3 | async-start | bytes 2097152 | tf_op jit(solution)/shard_map/all_to_all | solution.py:57
  121.3 9.6 %collective-permute-start.13 = (bf16[2,32,2048]{2,1,0:T(8,128)(2,1)S(1)}, bf16[2,32,2048]{2,1,0:T(8,128)(2,1)S(1)}, u32[]{:S(2)}, u32[]{:S(2)}) collective-permute-start(bf16[2,32,2048]{2,1,0:T(8,128)(2,1)S(1)} %pad_maximum_fusion.3.q0), channel_id=1, source_target_pairs={{0,64},{64,128},{128,192},{192,0},{1,65},{65,129},{129,193},{193,1... | collective-permute-start | bytes 786440 | tf_op jit(solution)/shard_map/ppermute | solution.py:331
  131.0 9.2 %collective-permute-done.14.q2 = bf16[2,32,2048]{2,1,0:T(8,128)(2,1)S(1)} collective-permute-done((bf16[2,32,2048]{2,1,0:T(8,128)(2,1)S(1)}, bf16[2,32,2048]{2,1,0:T(8,128)(2,1)S(1)}, u32[]{:S(2)}, u32[]{:S(2)}) %collective-permute-start.14) | collective-permute-done | bytes 262176 | tf_op jit(solution)/shard_map/ppermute | solution.py:331
  140.2 5.3 %collective-permute-done.13.q1 = bf16[2,32,2048]{2,1,0:T(8,128)(2,1)S(1)} collective-permute-done((bf16[2,32,2048]{2,1,0:T(8,128)(2,1)S(1)}, bf16[2,32,2048]{2,1,0:T(8,128)(2,1)S(1)}, u32[]{:S(2)}, u32[]{:S(2)}) %collective-permute-start.13) | collective-permute-done | bytes 262176 | tf_op jit(solution)/shard_map/ppermute | solution.py:331
  151.8 4.8 %all-to-all-start.4 = ((bf16[8,2,32,384]{3,2,1,0:T(8,128)(2,1)}), bf16[8,2,32,384]{3,2,1,0:T(8,128)(2,1)S(1)}, u32[]{:S(2)}, u32[]{:S(2)}) async-start(bf16[8,2,32,384]{3,2,1,0:T(8,128)(2,1)} %shard_map.156), calls=%async_computation.4 | async-start | bytes 786432 | tf_op jit(solution)/shard_map/all_to_all | solution.py:57
  164.0 5.8 %all-to-all-done.4.parts = bf16[8,2,32,384]{3,2,1,0:T(8,128)(2,1)S(1)} async-done(((bf16[8,2,32,384]{3,2,1,0:T(8,128)(2,1)}), bf16[8,2,32,384]{3,2,1,0:T(8,128)(2,1)S(1)}, u32[]{:S(2)}, u32[]{:S(2)}) %all-to-all-start.4) | async-done | bytes 393248 | tf_op jit(solution)/shard_map/all_to_all | solution.py:57
  172.2 5.8 %all-to-all-start.5 = ((f32[4,16,384]{2,1,0:T(8,128)}), f32[4,16,384]{2,1,0:T(8,128)S(1)}, u32[]{:S(2)}, u32[]{:S(2)}) async-start(f32[4,16,384]{2,1,0:T(8,128)} %bitcast.50), calls=%async_computation.5 | async-start | bytes 196608 | tf_op jit(solution)/shard_map/all_to_all | solution.py:57
  178.0 7.3 %shard_map.153 = bf16[128,2048]{1,0:T(8,128)(2,1)} custom-call(bf16[32,2048]{1,0:T(8,128)(2,1)} %shard_map.152.da_own, bf16[128,2048]{1,0:T(8,128)(2,1)} %bitcast.36, bf16[128,2048]{1,0:T(8,128)(2,1)} %bitcast.40, s32[1,32]{1,0:T(1,128)} %bitcast.63, f32[32,16]{1,0:T(8,128)} %get-tuple-element.91.cm, f32[16,128]{1,0:T(8,128)} %get-tuple-element.79.cum, ...), custom_call_target="tpu_custom_call" | custom-call | flops 100000000 | bytes 2771072 | tf_op jit(solution)/shard_map/pallas_call | solution.py:25
  185.3 4.1 %shard_map.154 = (f32[16,128,256]{2,1,0:T(8,128)}, bf16[16,128,256]{2,1,0:T(8,128)(2,1)}) custom-call(s32[5]{0:T(128)} %stack.56.ids, bf16[8,528,128]{2,1,0:T(8,128)(2,1)} %copy-done, bf16[2,32,2048]{2,1,0:T(8,128)(2,1)} %copy-done.3, bf16[2,32,2048]{2,1,0:T(8,128)(2,1)} %copy-done.8, bf16[2,32,2048]{2,1,0:T(8,128)(2,1)} %copy-done.7, ...), custom_call_target="tpu_custom_call" | custom-call | flops 100000000 | bytes 5808148 | tf_op jit(solution)/shard_map/pallas_call | solution.py:25
  190.4 6.2 %shard_map.155 = (bf16[128,2048]{1,0:T(8,128)(2,1)}, bf16[128,2048]{1,0:T(8,128)(2,1)}) custom-call(bf16[2,32,2048]{2,1,0:T(8,128)(2,1)} %copy-done.9, bf16[2,32,2048]{2,1,0:T(8,128)(2,1)} %copy-done.20, bf16[2,32,2048]{2,1,0:T(8,128)(2,1)} %copy-done.19, bf16[2,32,2048]{2,1,0:T(8,128)(2,1)} %copy-done.18, bf16[2,32,2048]{2,1,0:T(8,128)(2,1)} %copy-done.3, ...), custom_call_target="tpu_custom_call" | custom-call | flops 100000000 | bytes 6815744 | tf_op jit(solution)/shard_map/pallas_call | solution.py:25
  (120 shorter events, 55.3 us)
Async XLA Ops:
  7.6 24.0 %all-to-all-start = ((bf16[8,528,128]{2,1,0:T(8,128)(2,1)}), bf16[8,528,128]{2,1,0:T(8,128)(2,1)S(1)}, u32[]{:S(2)}, u32[]{:S(2)}) async-start(bf16[8,528,128]{2,1,0:T(8,128)(2,1)} %get-tuple-element.82), calls=%async_computation | async-start | bytes 2162688 | tf_op jit(solution)/shard_map/all_to_all | solution.py:57
  13.7 17.8 %collective-permute-start.3 = (bf16[1,32,2048]{2,1,0:T(8,128)(2,1)S(1)}, bf16[1,32,2048]{2,1,0:T(8,128)(2,1)S(1)}, u32[]{:S(2)}, u32[]{:S(2)}) collective-permute-start(bf16[1,32,2048]{2,1,0:T(8,128)(2,1)S(1)} %bitcast.66), channel_id=1, source_target_pairs={{0,1},{1,0},{2,3},{3,2},{4,5},{5,4},{6,7},{7,6},{8,9},{9,8},{10,11... | collective-permute-start | bytes 393224 | tf_op jit(solution)/shard_map/ppermute | solution.py:326
  17.4 12.3 %collective-permute-start.1 = (bf16[16,384]{1,0:T(8,128)(2,1)S(1)}, bf16[16,384]{1,0:T(8,128)(2,1)S(1)}, u32[]{:S(2)}, u32[]{:S(2)}) collective-permute-start(bf16[16,384]{1,0:T(8,128)(2,1)S(1)} %copy-done.30), channel_id=1, source_target_pairs={{0,32},{2,34},{32,0},{34,2},{1,33},{3,35},{33,1},{35,3},{4,36},{6,... | collective-permute-start | bytes 36872 | tf_op jit(solution)/shard_map/ppermute | solution.py:363
  18.5 13.0 %collective-permute-start.2 = (bf16[16,384]{1,0:T(8,128)(2,1)S(1)}, bf16[16,384]{1,0:T(8,128)(2,1)S(1)}, u32[]{:S(2)}, u32[]{:S(2)}) collective-permute-start(bf16[16,384]{1,0:T(8,128)(2,1)S(1)} %copy-done.29), channel_id=1, source_target_pairs={{0,34},{2,32},{32,2},{34,0},{1,35},{3,33},{33,3},{35,1},{4,38},{6,... | collective-permute-start | bytes 36872 | tf_op jit(solution)/shard_map/ppermute | solution.py:363
  35.2 24.3 %all-to-all-start.1 = ((bf16[8,512,128]{2,1,0:T(8,128)(2,1)}), bf16[8,512,128]{2,1,0:T(8,128)(2,1)S(1)}, u32[]{:S(2)}, u32[]{:S(2)}) async-start(bf16[8,512,128]{2,1,0:T(8,128)(2,1)} %shard_map.149), calls=%async_computation.1 | async-start | bytes 2097152 | tf_op jit(solution)/shard_map/all_to_all | solution.py:57
  41.0 14.2 %collective-permute-start.8 = (bf16[32,2048]{1,0:T(8,128)(2,1)S(1)}, bf16[32,2048]{1,0:T(8,128)(2,1)S(1)}, u32[]{:S(2)}, u32[]{:S(2)}) collective-permute-start(bf16[32,2048]{1,0:T(8,128)(2,1)S(1)} %copy-done.11), channel_id=1, source_target_pairs={{0,32},{32,0},{1,33},{33,1},{2,34},{34,2},{3,35},{35,3},{4,36},{36... | collective-permute-start | bytes 393224 | tf_op jit(solution)/shard_map/ppermute | solution.py:326
  45.6 13.9 %collective-permute-start.7 = (bf16[2,32,2048]{2,1,0:T(8,128)(2,1)S(1)}, bf16[2,32,2048]{2,1,0:T(8,128)(2,1)S(1)}, u32[]{:S(2)}, u32[]{:S(2)}) collective-permute-start(bf16[2,32,2048]{2,1,0:T(8,128)(2,1)S(1)} %pad_maximum_fusion.2), channel_id=1, source_target_pairs={{0,32},{32,0},{1,33},{33,1},{2,34},{34,2},{3,35},{35,3},{4,36},{36... | collective-permute-start | bytes 786440 | tf_op jit(solution)/shard_map/ppermute | solution.py:326
  47.9 10.4 %collective-permute-start.6 = (bf16[4,4,16,384]{3,2,1,0:T(8,128)(2,1)S(1)}, bf16[4,4,16,384]{3,2,1,0:T(8,128)(2,1)S(1)}, u32[]{:S(2)}, u32[]{:S(2)}) collective-permute-start(bf16[4,4,16,384]{3,2,1,0:T(8,128)(2,1)S(1)} %pad_maximum_fusion.5), channel_id=1, source_target_pairs={{0,16},{4,20},{8,24},{12,28},{16,0},{20,4},{24,8},{28,12},{1,17},{... | collective-permute-start | bytes 589832 | tf_op jit(solution)/shard_map/ppermute | solution.py:326
  64.4 35.9 %all-to-all-start.2 = ((bf16[8,32,2048]{2,1,0:T(8,128)(2,1)}), bf16[8,32,2048]{2,1,0:T(8,128)(2,1)S(1)}, u32[]{:S(2)}, u32[]{:S(2)}) async-start(bf16[8,32,2048]{2,1,0:T(8,128)(2,1)} %get-tuple-element.93), calls=%async_computation.2 | async-start | bytes 2097152 | tf_op jit(solution)/shard_map/all_to_all | solution.py:57
  75.5 24.9 %collective-permute-start.9 = (bf16[4,32,2048]{2,1,0:T(8,128)(2,1)S(1)}, bf16[4,32,2048]{2,1,0:T(8,128)(2,1)S(1)}, u32[]{:S(2)}, u32[]{:S(2)}) collective-permute-start(bf16[4,32,2048]{2,1,0:T(8,128)(2,1)S(1)} %pad_maximum_fusion), channel_id=1, source_target_pairs={{0,2},{2,0},{1,3},{3,1},{4,6},{6,4},{5,7},{7,5},{8,10},{10,8},{9,1... | collective-permute-start | bytes 1572872 | tf_op jit(solution)/shard_map/ppermute | solution.py:326
  75.6 13.3 %collective-permute-start.12 = (bf16[8,4,16,384]{3,2,1,0:T(8,128)(2,1)S(1)}, bf16[8,4,16,384]{3,2,1,0:T(8,128)(2,1)S(1)}, u32[]{:S(2)}, u32[]{:S(2)}) collective-permute-start(bf16[8,4,16,384]{3,2,1,0:T(8,128)(2,1)S(1)} %pad_maximum_fusion.1.w0), channel_id=1, source_target_pairs={{0,192},{64,0},{128,64},{192,128},{1,193},{65,1},{129,65},{193,129... | collective-permute-start | bytes 1179656 | tf_op jit(solution)/shard_map/ppermute | solution.py:331
  78.6 11.5 %collective-permute-start.11 = (bf16[8,4,16,384]{3,2,1,0:T(8,128)(2,1)S(1)}, bf16[8,4,16,384]{3,2,1,0:T(8,128)(2,1)S(1)}, u32[]{:S(2)}, u32[]{:S(2)}) collective-permute-start(bf16[8,4,16,384]{3,2,1,0:T(8,128)(2,1)S(1)} %pad_maximum_fusion.1.w0), channel_id=1, source_target_pairs={{0,128},{64,192},{128,0},{192,64},{1,129},{65,193},{129,1},{193,65... | collective-permute-start | bytes 1179656 | tf_op jit(solution)/shard_map/ppermute | solution.py:331
  81.5 18.0 %collective-permute-start.10 = (bf16[8,4,16,384]{3,2,1,0:T(8,128)(2,1)S(1)}, bf16[8,4,16,384]{3,2,1,0:T(8,128)(2,1)S(1)}, u32[]{:S(2)}, u32[]{:S(2)}) collective-permute-start(bf16[8,4,16,384]{3,2,1,0:T(8,128)(2,1)S(1)} %pad_maximum_fusion.1.w0), channel_id=1, source_target_pairs={{0,64},{64,128},{128,192},{192,0},{1,65},{65,129},{129,193},{193,1... | collective-permute-start | bytes 1179656 | tf_op jit(solution)/shard_map/ppermute | solution.py:331
  108.2 37.4 %all-to-all-start.3 = ((bf16[8,32,2048]{2,1,0:T(8,128)(2,1)}), bf16[8,32,2048]{2,1,0:T(8,128)(2,1)S(1)}, u32[]{:S(2)}, u32[]{:S(2)}) async-start(bf16[8,32,2048]{2,1,0:T(8,128)(2,1)} %get-tuple-element.105), calls=%async_computation.3 | async-start | bytes 2097152 | tf_op jit(solution)/shard_map/all_to_all | solution.py:57
  114.0 31.5 %collective-permute-start.16 = (bf16[512,384]{1,0:T(8,128)(2,1)}, bf16[512,384]{1,0:T(8,128)(2,1)S(1)}, u32[]{:S(2)}, u32[]{:S(2)}) collective-permute-start(bf16[512,384]{1,0:T(8,128)(2,1)} %get-tuple-element.102), channel_id=1, source_target_pairs={{0,64},{64,128},{128,192},{192,0},{1,65},{65,129},{129,193},{193,1... | collective-permute-start | bytes 1179656 | tf_op jit(solution)/shard_map/ppermute | solution.py:331
  114.9 30.6 %collective-permute-start.17 = (bf16[512,384]{1,0:T(8,128)(2,1)}, bf16[512,384]{1,0:T(8,128)(2,1)S(1)}, u32[]{:S(2)}, u32[]{:S(2)}) collective-permute-start(bf16[512,384]{1,0:T(8,128)(2,1)} %get-tuple-element.103), channel_id=1, source_target_pairs={{0,128},{64,192},{128,0},{192,64},{1,129},{65,193},{129,1},{193,65... | collective-permute-start | bytes 1179656 | tf_op jit(solution)/shard_map/ppermute | solution.py:331
  116.6 28.9 %collective-permute-start.18 = (bf16[512,384]{1,0:T(8,128)(2,1)}, bf16[512,384]{1,0:T(8,128)(2,1)S(1)}, u32[]{:S(2)}, u32[]{:S(2)}) collective-permute-start(bf16[512,384]{1,0:T(8,128)(2,1)} %get-tuple-element.104), channel_id=1, source_target_pairs={{0,192},{64,0},{128,64},{192,128},{1,193},{65,1},{129,65},{193,129... | collective-permute-start | bytes 1179656 | tf_op jit(solution)/shard_map/ppermute | solution.py:331
  118.7 21.5 %collective-permute-start.14 = (bf16[2,32,2048]{2,1,0:T(8,128)(2,1)S(1)}, bf16[2,32,2048]{2,1,0:T(8,128)(2,1)S(1)}, u32[]{:S(2)}, u32[]{:S(2)}) collective-permute-start(bf16[2,32,2048]{2,1,0:T(8,128)(2,1)S(1)} %pad_maximum_fusion.3.q0), channel_id=1, source_target_pairs={{0,128},{64,192},{128,0},{192,64},{1,129},{65,193},{129,1},{193,65... | collective-permute-start | bytes 786440 | tf_op jit(solution)/shard_map/ppermute | solution.py:331
  121.3 24.2 %collective-permute-start.13 = (bf16[2,32,2048]{2,1,0:T(8,128)(2,1)S(1)}, bf16[2,32,2048]{2,1,0:T(8,128)(2,1)S(1)}, u32[]{:S(2)}, u32[]{:S(2)}) collective-permute-start(bf16[2,32,2048]{2,1,0:T(8,128)(2,1)S(1)} %pad_maximum_fusion.3.q0), channel_id=1, source_target_pairs={{0,64},{64,128},{128,192},{192,0},{1,65},{65,129},{129,193},{193,1... | collective-permute-start | bytes 786440 | tf_op jit(solution)/shard_map/ppermute | solution.py:331
  151.8 18.0 %all-to-all-start.4 = ((bf16[8,2,32,384]{3,2,1,0:T(8,128)(2,1)}), bf16[8,2,32,384]{3,2,1,0:T(8,128)(2,1)S(1)}, u32[]{:S(2)}, u32[]{:S(2)}) async-start(bf16[8,2,32,384]{3,2,1,0:T(8,128)(2,1)} %shard_map.156), calls=%async_computation.4 | async-start | bytes 786432 | tf_op jit(solution)/shard_map/all_to_all | solution.py:57
  160.6 28.9 %collective-permute-start.22 = (bf16[2,32,2048]{2,1,0:T(8,128)(2,1)S(1)}, bf16[2,32,2048]{2,1,0:T(8,128)(2,1)S(1)}, u32[]{:S(2)}, u32[]{:S(2)}) collective-permute-start(bf16[2,32,2048]{2,1,0:T(8,128)(2,1)S(1)} %pad_maximum_fusion.4.a0), channel_id=1, source_target_pairs={{0,192},{64,0},{128,64},{192,128},{1,193},{65,1},{129,65},{193,129... | collective-permute-start | bytes 786440 | tf_op jit(solution)/shard_map/ppermute | solution.py:331
  161.5 28.0 %collective-permute-start.21 = (bf16[2,32,2048]{2,1,0:T(8,128)(2,1)S(1)}, bf16[2,32,2048]{2,1,0:T(8,128)(2,1)S(1)}, u32[]{:S(2)}, u32[]{:S(2)}) collective-permute-start(bf16[2,32,2048]{2,1,0:T(8,128)(2,1)S(1)} %pad_maximum_fusion.4.a0), channel_id=1, source_target_pairs={{0,128},{64,192},{128,0},{192,64},{1,129},{65,193},{129,1},{193,65... | collective-permute-start | bytes 786440 | tf_op jit(solution)/shard_map/ppermute | solution.py:331
  163.2 26.3 %collective-permute-start.20 = (bf16[2,32,2048]{2,1,0:T(8,128)(2,1)S(1)}, bf16[2,32,2048]{2,1,0:T(8,128)(2,1)S(1)}, u32[]{:S(2)}, u32[]{:S(2)}) collective-permute-start(bf16[2,32,2048]{2,1,0:T(8,128)(2,1)S(1)} %pad_maximum_fusion.4.a0), channel_id=1, source_target_pairs={{0,64},{64,128},{128,192},{192,0},{1,65},{65,129},{129,193},{193,1... | collective-permute-start | bytes 786440 | tf_op jit(solution)/shard_map/ppermute | solution.py:331
  172.2 24.4 %all-to-all-start.5 = ((f32[4,16,384]{2,1,0:T(8,128)}), f32[4,16,384]{2,1,0:T(8,128)S(1)}, u32[]{:S(2)}, u32[]{:S(2)}) async-start(f32[4,16,384]{2,1,0:T(8,128)} %bitcast.50), calls=%async_computation.5 | async-start | bytes 196608 | tf_op jit(solution)/shard_map/all_to_all | solution.py:57
  (37 other events, 513.4 us)
